TPU v7x, 256 devices: a whole 4x4x8 slice. The times are simulated.
256 devices in a mesh: mode: 16 (over z, core), dom: 16 (over y, x).
Axes of the slice: x: 4, y: 4, z: 8, core: 2. Of those that a mesh axis runs over, the one named last changes fastest.
Arguments:
- velocity: float32 [3, 128, 2, 32768], P(None, 'mode', None, 'dom'), may hold values from -0.375 to 0.375
- vorticity: float32 [3, 128, 2, 32768], P(None, 'mode', None, 'dom'), may hold values from -0.375 to 0.375
- blocks: float32 [9, 64, 64], replicated, may hold values from -0.042 to 0.042
- nbr_ref: int32 [9, 512], P(None, 'dom'), may hold values from 0 to 47
- send_list: int32 [2, 128], P(None, 'dom'), may hold values from 0 to 31
Outputs:
- velocity_new: float32 [3, 128, 2, 32768], P(None, 'mode', None, 'dom')
Inputs may be any that keep to these rules, and one draw needn't show every extreme that they name: nbr_ref indexes the extended list of the element's own partition; partitions form a cycle. send_list holds local element numbers of the partition that holds the entry.
All inputs are finite; a program needn't handle non-finite values.
Results may differ from a plain program's by a relative error of at most 0.0001.
Values sent between devices are 32-bit elements; how exact they have to be, the bound alone decides.
No kernel may reach another device: no remote copies, remote signals or barrier semaphores. Data moves between devices by JAX's collectives and lax.ppermute only.
A program may use at most 64 MiB of HBM per device.

v0:
```python
import functools

import jax
import jax.numpy as jnp
import numpy as np
from jax import lax
from jax.experimental import pallas as pl
from jax.experimental.pallas import tpu as pltpu
from jax.sharding import PartitionSpec as P

CHEB = 4
NP = 64
COMPS = 3
LANES = 128
bf16, f32 = jnp.bfloat16, jnp.float32


def split(value):
    high = value.astype(bf16)
    return high, (value - high.astype(f32)).astype(bf16)


def np_split(value):
    high = value.astype(np.float32).astype(bf16)
    return high, (value - high.astype(np.float64)).astype(np.float32).astype(bf16)


def spanwise_tables(count):
    planes = 2 * count
    angle = 2 * np.pi / planes * ((np.arange(planes)[:, None] * np.arange(count)[None, :]) % planes)
    weights = np.where(np.arange(count) == 0, 1.0, 2.0)
    forward = np.stack([weights * np.cos(angle), -weights * np.sin(angle)], axis=2).reshape(planes, planes)
    back = np.stack([np.cos(angle).T, -np.sin(angle).T], axis=1).reshape(planes, planes) / planes
    return np_split(forward) + np_split(back)


def dot(a, b):
    return jnp.dot(a, b, preferred_element_type=f32)


def dot3(a, b):
    return dot(a[0], b[0]) + dot(a[1], b[0]) + dot(a[0], b[1])


def lines_kernel(lines, table, fwd_hi, fwd_lo, back_hi, back_lo, out):
    senders, rows, _ = lines.shape
    per = rows // (2 * COMPS)
    count = senders * per
    fields = [lines[:, i * per:(i + 1) * per, :].reshape(count, LANES) for i in range(2 * COMPS)]
    forward = (fwd_hi[...], fwd_lo[...])
    planes = [dot3(forward, split(jnp.concatenate(fields[i:i + 2], axis=1))) for i in range(0, 2 * COMPS, 2)]
    planes = [half for pair in planes for half in (pair[:, :LANES], pair[:, LANES:])]
    u, w = planes[:COMPS], planes[COMPS:]
    cross = jnp.concatenate([u[(c + 1) % 3] * w[(c + 2) % 3] - u[(c + 2) % 3] * w[(c + 1) % 3] for c in range(3)], axis=1)
    forcing = dot3((back_hi[...], back_lo[...]), split(cross))
    mode = lax.broadcasted_iota(jnp.int32, (count, LANES), 0) >> 1
    wavenum = mode.astype(f32) * (2.0 / count)
    inv_diag = 1.0 / (1.0 + 4.0 * wavenum * wavenum)
    for c in range(COMPS):
        out[:, 0, c * LANES:(c + 1) * LANES] = (fields[c] + forcing[:, c * LANES:(c + 1) * LANES]) * inv_diag
    out[:, 0, COMPS * LANES:] = jnp.broadcast_to(table[...], (count, LANES))


def solve_kernel(parts, pairs, slots, send, scal, state_in, w_hi, w_lo, out,
                 onehot, ext_hi, ext_lo, y_hi, y_lo, sol, resid, dirn, kap):
    elems = 2 * pairs
    half = lax.broadcasted_iota(jnp.int32, (parts * pairs, LANES), 1) < NP
    x = [state_in[:, c * LANES:(c + 1) * LANES] for c in range(COMPS)]
    swap = [pltpu.roll(v, NP, 1) for v in x]
    shape = (parts, pairs, LANES)
    zero = jnp.zeros_like(x[0])
    dirn[:, 0, :, :LANES] = jnp.where(half, x[0], swap[1]).reshape(shape)
    dirn[:, 0, :, LANES:] = jnp.where(half, x[2], zero).reshape(shape)
    dirn[:, 1, :, :LANES] = jnp.where(half, swap[0], x[1]).reshape(shape)
    dirn[:, 1, :, LANES:] = jnp.where(half, swap[2], zero).reshape(shape)
    resid[...] = dirn[...]
    sol[...] = jnp.zeros_like(sol)

    refs = state_in[:, COMPS * LANES:]
    below = jnp.concatenate([refs[-pairs:], refs[:-pairs]], axis=0)
    above = jnp.concatenate([refs[pairs:], refs[:pairs]], axis=0)
    local = refs
    first = 2 * slots
    for s in range(send):
        local = jnp.where(refs == float(elems + s), below[:, first + s:first + s + 1], local)
        at = first + send + s
        local = jnp.where(refs == float(elems + send + s), above[:, at:at + 1], local)
    local = local.astype(jnp.int32)
    place = jnp.where(refs < float(elems), elems, jnp.where(refs < float(elems + send), 0, 2 * elems))
    kap[...] = place + (local & 1) * pairs + (local >> 1)

    lane = lax.broadcasted_iota(jnp.int32, (pairs, 2 * LANES), 1)
    lane = jnp.where(lane >= 3 * elems, lane - 3 * elems, lane)
    lane = jnp.where(lax.broadcasted_iota(jnp.int32, lane.shape, 1) < 6 * elems, lane, -1)

    def build(d, carry):
        rows = kap[pl.ds(pl.multiple_of(d * pairs, pairs), pairs), :]
        for s in range(slots):
            for h in range(2):
                col = rows[:, h * slots + s:h * slots + s + 1]
                hit = jnp.where(lane == col, 1.0, 0.0).astype(bf16)
                onehot[d, s * elems + h * pairs:s * elems + (h + 1) * pairs, :] = hit
        return carry

    lax.fori_loop(0, parts, build, 0)
    inv_diag = scal[0]
    total_rows = parts * elems

    def step(i, carry):
        now = dirn[...].reshape(total_rows, 2 * LANES)
        hi, lo = split(now)
        for ext, val in ((ext_hi, hi), (ext_lo, lo)):
            ext[elems:elems + total_rows] = val
            ext[:elems] = val[total_rows - elems:]
            ext[elems + total_rows:] = val[:elems]

        def gather(d, c):
            at = pl.ds(pl.multiple_of(d * elems, elems), 3 * elems)
            window = jnp.concatenate([ext_hi[at], ext_lo[at], jnp.zeros((2 * LANES - 6 * elems, 2 * LANES), bf16)], axis=0)
            y = dot(onehot[d], window)
            hi, lo = split(y)
            to = pl.ds(pl.multiple_of(d * elems, elems), elems)
            for s in range(slots):
                y_hi[s, to, :] = hi[s * elems:(s + 1) * elems]
                y_lo[s, to, :] = lo[s * elems:(s + 1) * elems]
            return c

        lax.fori_loop(0, parts, gather, 0)
        total = jnp.zeros((total_rows, 2 * LANES), f32)
        yh = jnp.concatenate([y_hi[s] for s in range(slots)], axis=1)
        yl = jnp.concatenate([y_lo[s] for s in range(slots)], axis=1)
        total = dot(yh, w_hi[...]) + dot(yl, w_hi[...]) + dot(yh, w_lo[...])
        total = total.reshape(dirn.shape)
        old = dirn[...]
        sol[...] = sol[...] + old
        left = resid[...] - (old + inv_diag * total)
        resid[...] = left
        dirn[...] = scal[1 + 2 * i] * old + scal[2 + 2 * i] * left
        return carry

    lax.fori_loop(0, CHEB, step, 0)
    final = sol[...] + dirn[...]
    f = [final[:, h].reshape(parts * pairs, 2 * LANES) for h in range(2)]
    a, b = [v[:, :LANES] for v in f], [v[:, LANES:] for v in f]
    out[:, 0] = jnp.where(half, a[0], pltpu.roll(a[1], NP, 1)).reshape(shape)
    out[:, 1] = jnp.where(half, pltpu.roll(a[0], NP, 1), a[1]).reshape(shape)
    out[:, 2] = jnp.where(half, b[0], pltpu.roll(b[1], NP, 1)).reshape(shape)


def vmem(n):
    return [pl.BlockSpec(memory_space=pltpu.VMEM)] * n


def shards(velocity, vorticity, blocks, nbr_ref, send_list):
    comps, modes_dev, _, merged = velocity.shape
    n_mode, parts = lax.axis_size("mode"), lax.axis_size("dom")
    slots, elems = nbr_ref.shape
    send = send_list.shape[1]
    pairs = elems // 2
    modes_all = modes_dev * n_mode
    me = lax.axis_index("mode")
    rows = comps * modes_dev * 2

    both = jnp.concatenate([v.reshape(rows, n_mode, LANES) for v in (velocity, vorticity)], axis=0)
    lines = lax.all_to_all(both.transpose(1, 0, 2), "mode", split_axis=0, concat_axis=0, tiled=True)

    mine = lax.dynamic_slice_in_dim(nbr_ref.reshape(slots, pairs, 2), me, 1, axis=1)[:, 0]
    table = jnp.concatenate([mine.T.reshape(-1), send_list.reshape(-1)]).astype(f32)
    table = jnp.pad(table, (0, LANES - table.shape[0])).reshape(1, LANES)
    width = (comps + 1) * LANES
    devices = n_mode * parts
    rhs = pl.pallas_call(
        lines_kernel,
        out_shape=jax.ShapeDtypeStruct((devices, 1, width), f32),
        in_specs=vmem(6), out_specs=vmem(1)[0], name="lines",
    )(lines, table, *[jnp.asarray(t) for t in spanwise_tables(modes_all)])
    columns = lax.all_to_all(rhs, ("mode", "dom"), split_axis=0, concat_axis=0, tiled=True)
    columns = columns.reshape(n_mode, parts, width).transpose(1, 0, 2).reshape(devices, width)

    eye = jnp.eye(4, dtype=f32).at[3, 3].set(0.0)
    weight = jnp.einsum("spq,cd->scqdp", blocks, eye).reshape(slots * 4 * NP, 4 * NP)
    rounded = lax.reduce_precision(weight, 8, 7)
    w_hi, w_lo = rounded.astype(bf16), (weight - rounded).astype(bf16)
    mode = me * modes_dev + lax.axis_index("dom") // 2
    wavenum = mode.astype(f32) / modes_all
    coefs = []
    rho = 0.5
    for _ in range(CHEB):
        rho_next = 1.0 / (4.0 - rho)
        coefs += [rho_next * rho, 4.0 * rho_next]
        rho = rho_next
    scal = jnp.concatenate([(1.0 / (1.0 + 4.0 * wavenum * wavenum)).reshape(1), jnp.asarray(coefs, f32)])
    state = pltpu.VMEM((parts, 2, pairs, 2 * LANES), f32)
    ext = pltpu.VMEM(((parts + 2) * elems, 2 * LANES), bf16)
    picked = pltpu.VMEM((slots, parts * elems, 2 * LANES), bf16)
    done = pl.pallas_call(
        functools.partial(solve_kernel, parts, pairs, slots, send),
        out_shape=jax.ShapeDtypeStruct((parts, comps, pairs, LANES), f32),
        in_specs=[pl.BlockSpec(memory_space=pltpu.SMEM)] + vmem(3), out_specs=vmem(1)[0],
        scratch_shapes=[
            pltpu.VMEM((parts, slots * elems, 2 * LANES), bf16), ext, ext, picked, picked,
            state, state, state, pltpu.VMEM((devices, LANES), jnp.int32),
        ],
        name="solve",
    )(scal, columns, w_hi, w_lo)
    back = lax.all_to_all(done.reshape(parts, comps * pairs, LANES), "dom", split_axis=0, concat_axis=0, tiled=True)
    back = back.reshape(modes_dev, 2, comps, pairs, LANES).transpose(2, 0, 1, 3, 4)
    return back.reshape(comps, modes_dev, 2, merged)


def solution(mesh):
    placed = (
        P(None, "mode", None, "dom"),
        P(None, "mode", None, "dom"),
        P(),
        P(None, "dom"),
        P(None, "dom"),
    )
    return jax.shard_map(
        shards, mesh=mesh, in_specs=placed, out_specs=P(None, "mode", None, "dom"), check_vma=False
    )
```

profile of v0, /device:TPU:1, one launch (start us, length us, event | category | flops | bytes accessed | tf_op | source)
XLA Modules:
  0.0 111.5 jit_solution(11043521741073526434)
XLA Ops:
  0.0 1.3 %reshape.69 = f32[48,16,128]{2,1,0:T(8,128)S(1)} reshape(f32[3,8,2,2048]{3,2,1,0:T(2,128)} %param.12) | data formatting | bytes 786432 | tf_op jit(solution)/shard_map/reshape | solution.py:164
  1.3 0.1 copy.15
  1.5 0.0 copy-start.3
  1.5 0.0 copy-start.2
  1.5 0.0 copy-start.1
  1.5 1.4 %reshape.70 = f32[48,16,128]{2,1,0:T(8,128)S(1)} reshape(f32[3,8,2,2048]{3,2,1,0:T(2,128)} %param.13) | data formatting | bytes 786432 | tf_op jit(solution)/shard_map/reshape | solution.py:164
  2.8 0.1 copy.16
  3.0 1.0 maximum_bitcast_fusion
  4.0 10.0 %all-to-all-start = ((f32[16,96,128]{2,1,0:T(8,128)}), f32[16,96,128]{2,1,0:T(8,128)S(1)}, u32[]{:S(2)}, u32[]{:S(2)}) async-start(f32[16,96,128]{2,1,0:T(8,128)} %maximum_bitcast_fusion), calls=%async_computation | async-start | bytes 1572864 | tf_op jit(solution)/shard_map/all_to_all | solution.py:165
  13.9 0.0 copy-done.3
  13.9 0.1 reshape.73
  14.0 0.0 copy-done.2
  14.0 0.1 copy.17
  14.1 0.1 reshape.72
  14.2 0.0 copy-done.1
  14.2 0.1 copy.19
  14.3 0.1 scatter.4
  14.5 0.1 add_convert_fusion
  14.5 0.5 pad_bitcast_fusion.table
  15.1 21.6 %all-to-all-done.lines = f32[16,96,128]{2,1,0:T(8,128)S(1)} async-done(((f32[16,96,128]{2,1,0:T(8,128)}), f32[16,96,128]{2,1,0:T(8,128)S(1)}, u32[]{:S(2)}, u32[]{:S(2)}) %all-to-all-start) | async-done | bytes 786464 | tf_op jit(solution)/shard_map/all_to_all | solution.py:165
  36.6 0.0 copy-start
  36.6 0.9 copy-done
  37.5 3.2 %lines.1 = f32[256,1,512]{2,1,0:T(1,128)} custom-call(f32[16,96,128]{2,1,0:T(8,128)} %copy-done, f32[1,128]{1,0:T(1,128)} %pad_bitcast_fusion.table, bf16[256,256]{1,0:T(8,128)(2,1)} %constant.77.clone.fwd_hi, bf16[256,256]{1,0:T(8,128)(2,1)} %constant.78.clone.fwd_lo, bf16[256,256]{1,0:T(8,128)(2,1)} %constant.79.clone.back_hi, ...), custom_call_target="tpu_custom_call" | custom-call | tf_op jit(solution)/shard_map/lines/pallas_call | solution.py:172
  40.8 8.8 %all-to-all-start.1 = ((f32[256,1,512]{2,1,0:T(1,128)}), f32[256,1,512]{2,1,0:T(1,128)S(1)}, u32[]{:S(2)}, u32[]{:S(2)}) async-start(f32[256,1,512]{2,1,0:T(1,128)} %lines.1), calls=%async_computation.1 | async-start | bytes 1048576 | tf_op jit(solution)/shard_map/all_to_all | solution.py:177
  49.5 3.3 %multiply_bitcast_fusion = f32[9,4,64,4,64]{4,3,2,1,0:T(4,128)} fusion(f32[9,64,64]{1,2,0:T(8,128)S(1)} %copy.19, f32[4,4]{1,0:T(4,128)S(1)} %scatter.4), kind=kLoop, calls=%fused_computation | loop fusion | flops 589824 | bytes 2506816 | tf_op jit(solution)/shard_map/spq,cd->scqdp/transpose | solution.py:181
  52.9 0.0 copy-start.4
  52.9 4.5 %reshape.77 = f32[2304,256]{1,0:T(8,128)S(1)} reshape(f32[9,4,64,4,64]{4,3,2,1,0:T(4,128)} %multiply_bitcast_fusion) | data formatting | bytes 4718592 | tf_op jit(solution)/shard_map/reshape | solution.py:181
  57.4 0.0 copy-done.4
  57.4 0.6 pad_maximum_fusion.scal
  58.0 1.8 %fusion = (bf16[2304,256]{1,0:T(8,128)(2,1)}, bf16[2304,256]{1,0:T(8,128)(2,1)}) fusion(f32[2304,256]{1,0:T(8,128)S(1)} %reshape.77), kind=kLoop, calls=%fused_computation.3 | loop fusion | flops 2359296 | bytes 4718592 | tf_op jit(solution)/shard_map/convert_element_type | solution.py:183
  59.7 10.6 %all-to-all-done.1 = f32[256,1,512]{2,1,0:T(1,128)S(1)} async-done(((f32[256,1,512]{2,1,0:T(1,128)}), f32[256,1,512]{2,1,0:T(1,128)S(1)}, u32[]{:S(2)}, u32[]{:S(2)}) %all-to-all-start.1) | async-done | bytes 524320 | tf_op jit(solution)/shard_map/all_to_all | solution.py:177
  70.4 1.1 copy.18
  71.5 25.9 %solve.1 = f32[16,3,16,128]{3,2,1,0:T(8,128)} custom-call(f32[9]{0:T(128)} %pad_maximum_fusion.scal, f32[256,512]{1,0:T(8,128)} %bitcast.24, bf16[2304,256]{1,0:T(8,128)(2,1)} %get-tuple-element.18.w_hi, bf16[2304,256]{1,0:T(8,128)(2,1)} %get-tuple-element.17.w_lo), custom_call_target="tpu_custom_call" | custom-call | tf_op jit(solution)/shard_map/solve/pallas_call | solution.py:196
  97.4 13.0 %all_to_all.15 = f32[16,48,128]{2,1,0:T(8,128)S(1)} all-to-all(f32[16,48,128]{2,1,0:T(8,128)} %bitcast.27), channel_id=1, replica_groups=mesh['mode'=16,'dom'=16] {'dom'}, dimensions={0} | all-to-all | bytes 786432 | tf_op jit(solution)/shard_map/all_to_all | solution.py:206
  110.5 1.0 reshape.80
  (4 shorter events, 0.1 us)
Async XLA Ops:
  1.5 12.5 %copy-start.3 = (s32[2,8]{1,0:T(2,128)S(1)}, s32[2,8]{1,0:T(2,128)}, u32[]{:S(2)}) copy-start(s32[2,8]{1,0:T(2,128)} %param.16) | copy-start | bytes 196
  1.5 12.5 %copy-start.2 = (s32[9,32]{1,0:T(8,128)S(1)}, s32[9,32]{1,0:T(8,128)}, u32[]{:S(2)}) copy-start(s32[9,32]{1,0:T(8,128)} %param.15) | copy-start | bytes 3460
  1.5 12.7 %copy-start.1 = (f32[9,64,64]{2,1,0:T(8,128)S(1)}, f32[9,64,64]{2,1,0:T(8,128)}, u32[]{:S(2)}) copy-start(f32[9,64,64]{2,1,0:T(8,128)} %param.14) | copy-start | bytes 442372
  4.0 32.7 %all-to-all-start = ((f32[16,96,128]{2,1,0:T(8,128)}), f32[16,96,128]{2,1,0:T(8,128)S(1)}, u32[]{:S(2)}, u32[]{:S(2)}) async-start(f32[16,96,128]{2,1,0:T(8,128)} %maximum_bitcast_fusion), calls=%async_computation | async-start | bytes 1572864 | tf_op jit(solution)/shard_map/all_to_all | solution.py:165
  36.6 0.9 copy-start
  40.8 29.6 %all-to-all-start.1 = ((f32[256,1,512]{2,1,0:T(1,128)}), f32[256,1,512]{2,1,0:T(1,128)S(1)}, u32[]{:S(2)}, u32[]{:S(2)}) async-start(f32[256,1,512]{2,1,0:T(1,128)} %lines.1), calls=%async_computation.1 | async-start | bytes 1048576 | tf_op jit(solution)/shard_map/all_to_all | solution.py:177
  52.9 4.5 %copy-start.4 = (f32[8]{0:T(128)S(1)}, f32[8]{0:T(128)}, u32[]{:S(2)}) copy-start(f32[8]{0:T(128)} %constant.81.clone) | copy-start | bytes 100
where the time goes:
time: 112 us; the launch traced here: 111 us
  waiting for transfers between devices  32.2 us (29%)
  Pallas kernels  29.2 us (26%)
  starting transfers between devices  18.7 us (17%)
  blocking collectives  13 us (12%)
  local copies, waits for them, and re-layouts  11.5 us (10%)
  other arithmetic  6.71 us (6%)
    pallas_call x1, Pallas kernels, shards(): pl.pallas_call(functools.partial(solve_kernel, parts, pairs, slots, send)...  25.9 us
    all_to_all x1, waiting for transfers between devices, shards(): lax.all_to_all(both.transpose(1, 0, 2), 'mode', split_axis=0, concat_axis...  21.6 us
    all_to_all x1, blocking collectives, shards(): lax.all_to_all(done.reshape(parts, comps * pairs, LANES), 'dom', split_ax...  13 us
    all_to_all x1, waiting for transfers between devices, shards(): lax.all_to_all(rhs, ('mode', 'dom'), split_axis=0, concat_axis=0, tiled=T...  10.6 us
    all_to_all x1, starting transfers between devices, shards(): lax.all_to_all(both.transpose(1, 0, 2), 'mode', split_axis=0, concat_axis...  9.97 us
    all_to_all x1, starting transfers between devices, shards(): lax.all_to_all(rhs, ('mode', 'dom'), split_axis=0, concat_axis=0, tiled=T...  8.76 us
    reshape x1, local copies, waits for them, and re-layouts, shards(): jnp.einsum('spq,cd->scqdp', blocks, eye).reshape(slots * 4 * NP, 4 * NP)  4.48 us
    transpose x1, other arithmetic, shards(): jnp.einsum('spq,cd->scqdp', blocks, eye).reshape(slots * 4 * NP, 4 * NP)  3.29 us
  transfers between devices with their start and end apart: 2, of which 2 were waited for; matrix products, arithmetic and copies ran while one was open for 10% of the time, Pallas kernels for 0%

commit v1 on v0

--- a/solution.py
+++ b/solution.py
@@ -8,6 +8,7 @@
 from jax.experimental.pallas import tpu as pltpu
 from jax.sharding import PartitionSpec as P
 
+
 CHEB = 4
 NP = 64
 COMPS = 3
@@ -31,7 +32,7 @@
     weights = np.where(np.arange(count) == 0, 1.0, 2.0)
     forward = np.stack([weights * np.cos(angle), -weights * np.sin(angle)], axis=2).reshape(planes, planes)
     back = np.stack([np.cos(angle).T, -np.sin(angle).T], axis=1).reshape(planes, planes) / planes
-    return np_split(forward) + np_split(back)
+    return np.stack(np_split(forward) + np_split(back))
 
 
 def dot(a, b):
@@ -42,27 +43,73 @@
     return dot(a[0], b[0]) + dot(a[1], b[0]) + dot(a[0], b[1])
 
 
-def lines_kernel(lines, table, fwd_hi, fwd_lo, back_hi, back_lo, out):
+def lines_kernel(lines, tables, out):
     senders, rows, _ = lines.shape
     per = rows // (2 * COMPS)
     count = senders * per
     fields = [lines[:, i * per:(i + 1) * per, :].reshape(count, LANES) for i in range(2 * COMPS)]
-    forward = (fwd_hi[...], fwd_lo[...])
+    forward = (tables[0], tables[1])
     planes = [dot3(forward, split(jnp.concatenate(fields[i:i + 2], axis=1))) for i in range(0, 2 * COMPS, 2)]
     planes = [half for pair in planes for half in (pair[:, :LANES], pair[:, LANES:])]
     u, w = planes[:COMPS], planes[COMPS:]
     cross = jnp.concatenate([u[(c + 1) % 3] * w[(c + 2) % 3] - u[(c + 2) % 3] * w[(c + 1) % 3] for c in range(3)], axis=1)
-    forcing = dot3((back_hi[...], back_lo[...]), split(cross))
+    forcing = dot3((tables[2], tables[3]), split(cross))
     mode = lax.broadcasted_iota(jnp.int32, (count, LANES), 0) >> 1
     wavenum = mode.astype(f32) * (2.0 / count)
     inv_diag = 1.0 / (1.0 + 4.0 * wavenum * wavenum)
     for c in range(COMPS):
         out[:, 0, c * LANES:(c + 1) * LANES] = (fields[c] + forcing[:, c * LANES:(c + 1) * LANES]) * inv_diag
-    out[:, 0, COMPS * LANES:] = jnp.broadcast_to(table[...], (count, LANES))
-
-
-def solve_kernel(parts, pairs, slots, send, scal, state_in, w_hi, w_lo, out,
-                 onehot, ext_hi, ext_lo, y_hi, y_lo, sol, resid, dirn, kap):
+
+
+def prep_kernel(parts, pairs, slots, send, table, onehot, kap):
+    elems = 2 * pairs
+    refs = table[...]
+    below = jnp.concatenate([refs[-pairs:], refs[:-pairs]], axis=0)
+    above = jnp.concatenate([refs[pairs:], refs[:pairs]], axis=0)
+    local = refs
+    first = 2 * slots
+    for s in range(send):
+        local = jnp.where(refs == float(elems + s), below[:, first + s:first + s + 1], local)
+        at = first + send + s
+        local = jnp.where(refs == float(elems + send + s), above[:, at:at + 1], local)
+    local = local.astype(jnp.int32)
+    place = jnp.where(refs < float(elems), elems, jnp.where(refs < float(elems + send), 0, 2 * elems))
+    kap[...] = place + (local & 1) * pairs + (local >> 1)
+
+    lane = lax.broadcasted_iota(jnp.int32, (pairs, 2 * LANES), 1)
+    lane = jnp.where(lane >= 3 * elems, lane - 3 * elems, lane)
+    lane = jnp.where(lax.broadcasted_iota(jnp.int32, lane.shape, 1) < 6 * elems, lane, -1)
+
+    def build(d, carry):
+        rows = kap[pl.ds(pl.multiple_of(d * pairs, pairs), pairs), :]
+        for s in range(slots):
+            for h in range(2):
+                col = rows[:, h * slots + s:h * slots + s + 1]
+                hit = jnp.where(lane == col, 1.0, 0.0).astype(bf16)
+                onehot[d, s * elems + h * pairs:s * elems + (h + 1) * pairs, :] = hit
+        return carry
+
+    lax.fori_loop(0, parts, build, 0)
+
+
+def weight_kernel(slots, blocks, w_hi, w_lo):
+    w_hi[...] = jnp.zeros_like(w_hi)
+    w_lo[...] = jnp.zeros_like(w_lo)
+
+    def place_block(s, carry):
+        hi, lo = split(blocks[s].T)
+        base = pl.multiple_of(s * 4 * NP, 4 * NP)
+        for c in range(COMPS):
+            at = (pl.ds(base + c * NP, NP), slice(c * NP, (c + 1) * NP))
+            w_hi[at] = hi
+            w_lo[at] = lo
+        return carry
+
+    lax.fori_loop(0, slots, place_block, 0)
+
+
+def solve_kernel(parts, pairs, slots, scal, state_in, onehot, w_hi, w_lo, out,
+                 ext_hi, ext_lo, y_hi, y_lo, sol, resid, dirn):
     elems = 2 * pairs
     half = lax.broadcasted_iota(jnp.int32, (parts * pairs, LANES), 1) < NP
     x = [state_in[:, c * LANES:(c + 1) * LANES] for c in range(COMPS)]
@@ -76,33 +123,6 @@
     resid[...] = dirn[...]
     sol[...] = jnp.zeros_like(sol)
 
-    refs = state_in[:, COMPS * LANES:]
-    below = jnp.concatenate([refs[-pairs:], refs[:-pairs]], axis=0)
-    above = jnp.concatenate([refs[pairs:], refs[:pairs]], axis=0)
-    local = refs
-    first = 2 * slots
-    for s in range(send):
-        local = jnp.where(refs == float(elems + s), below[:, first + s:first + s + 1], local)
-        at = first + send + s
-        local = jnp.where(refs == float(elems + send + s), above[:, at:at + 1], local)
-    local = local.astype(jnp.int32)
-    place = jnp.where(refs < float(elems), elems, jnp.where(refs < float(elems + send), 0, 2 * elems))
-    kap[...] = place + (local & 1) * pairs + (local >> 1)
-
-    lane = lax.broadcasted_iota(jnp.int32, (pairs, 2 * LANES), 1)
-    lane = jnp.where(lane >= 3 * elems, lane - 3 * elems, lane)
-    lane = jnp.where(lax.broadcasted_iota(jnp.int32, lane.shape, 1) < 6 * elems, lane, -1)
-
-    def build(d, carry):
-        rows = kap[pl.ds(pl.multiple_of(d * pairs, pairs), pairs), :]
-        for s in range(slots):
-            for h in range(2):
-                col = rows[:, h * slots + s:h * slots + s + 1]
-                hit = jnp.where(lane == col, 1.0, 0.0).astype(bf16)
-                onehot[d, s * elems + h * pairs:s * elems + (h + 1) * pairs, :] = hit
-        return carry
-
-    lax.fori_loop(0, parts, build, 0)
     inv_diag = scal[0]
     total_rows = parts * elems
 
@@ -125,8 +145,7 @@
                 y_lo[s, to, :] = lo[s * elems:(s + 1) * elems]
             return c
 
-        lax.fori_loop(0, parts, gather, 0)
-        total = jnp.zeros((total_rows, 2 * LANES), f32)
+        lax.fori_loop(0, parts, gather, 0, unroll=4)
         yh = jnp.concatenate([y_hi[s] for s in range(slots)], axis=1)
         yl = jnp.concatenate([y_lo[s] for s in range(slots)], axis=1)
         total = dot(yh, w_hi[...]) + dot(yl, w_hi[...]) + dot(yh, w_lo[...])
@@ -164,23 +183,45 @@
     both = jnp.concatenate([v.reshape(rows, n_mode, LANES) for v in (velocity, vorticity)], axis=0)
     lines = lax.all_to_all(both.transpose(1, 0, 2), "mode", split_axis=0, concat_axis=0, tiled=True)
 
-    mine = lax.dynamic_slice_in_dim(nbr_ref.reshape(slots, pairs, 2), me, 1, axis=1)[:, 0]
-    table = jnp.concatenate([mine.T.reshape(-1), send_list.reshape(-1)]).astype(f32)
-    table = jnp.pad(table, (0, LANES - table.shape[0])).reshape(1, LANES)
-    width = (comps + 1) * LANES
+    table = jnp.concatenate([
+        nbr_ref.reshape(slots, pairs, 2).transpose(1, 2, 0).reshape(pairs, 2 * slots),
+        jnp.broadcast_to(send_list.reshape(1, 2 * send), (pairs, 2 * send)),
+    ], axis=1).astype(f32)
+    table = jnp.pad(table, ((0, 0), (0, LANES - table.shape[1])))
+    side = 4
+    near = [[a * side + b for b in range(side)] for a in range(parts // side)]
+    far = [[a * side + b for a in range(parts // side)] for b in range(side)]
+    table = lax.all_gather(table, "dom", axis=0, tiled=True, axis_index_groups=near)
+    table = lax.all_gather(table, "dom", axis=0, tiled=True, axis_index_groups=far)
+    onehot = pl.pallas_call(
+        functools.partial(prep_kernel, parts, pairs, slots, send),
+        out_shape=jax.ShapeDtypeStruct((parts, slots * elems, 2 * LANES), bf16),
+        in_specs=vmem(1), out_specs=vmem(1)[0],
+        scratch_shapes=[pltpu.VMEM((parts * pairs, LANES), jnp.int32)],
+        compiler_params=pltpu.CompilerParams(vmem_limit_bytes=12 << 20),
+        cost_estimate=pl.CostEstimate(flops=0, bytes_accessed=12 << 20, transcendentals=0),
+        name="prep",
+    )(table)
+
+    width = comps * LANES
     devices = n_mode * parts
     rhs = pl.pallas_call(
         lines_kernel,
         out_shape=jax.ShapeDtypeStruct((devices, 1, width), f32),
-        in_specs=vmem(6), out_specs=vmem(1)[0], name="lines",
-    )(lines, table, *[jnp.asarray(t) for t in spanwise_tables(modes_all)])
+        in_specs=vmem(2), out_specs=vmem(1)[0], name="lines",
+        compiler_params=pltpu.CompilerParams(vmem_limit_bytes=12 << 20),
+    )(lines, jnp.asarray(spanwise_tables(modes_all)))
     columns = lax.all_to_all(rhs, ("mode", "dom"), split_axis=0, concat_axis=0, tiled=True)
+    weight = jax.ShapeDtypeStruct((slots * 4 * NP, 4 * NP), bf16)
+    w_hi, w_lo = pl.pallas_call(
+        functools.partial(weight_kernel, slots), out_shape=[weight, weight],
+        in_specs=vmem(1), out_specs=vmem(2),
+        compiler_params=pltpu.CompilerParams(vmem_limit_bytes=6 << 20),
+        cost_estimate=pl.CostEstimate(flops=0, bytes_accessed=3 << 20, transcendentals=0),
+        name="weights",
+    )(blocks)
     columns = columns.reshape(n_mode, parts, width).transpose(1, 0, 2).reshape(devices, width)
 
-    eye = jnp.eye(4, dtype=f32).at[3, 3].set(0.0)
-    weight = jnp.einsum("spq,cd->scqdp", blocks, eye).reshape(slots * 4 * NP, 4 * NP)
-    rounded = lax.reduce_precision(weight, 8, 7)
-    w_hi, w_lo = rounded.astype(bf16), (weight - rounded).astype(bf16)
     mode = me * modes_dev + lax.axis_index("dom") // 2
     wavenum = mode.astype(f32) / modes_all
     coefs = []
@@ -194,15 +235,13 @@
     ext = pltpu.VMEM(((parts + 2) * elems, 2 * LANES), bf16)
     picked = pltpu.VMEM((slots, parts * elems, 2 * LANES), bf16)
     done = pl.pallas_call(
-        functools.partial(solve_kernel, parts, pairs, slots, send),
+        functools.partial(solve_kernel, parts, pairs, slots),
         out_shape=jax.ShapeDtypeStruct((parts, comps, pairs, LANES), f32),
-        in_specs=[pl.BlockSpec(memory_space=pltpu.SMEM)] + vmem(3), out_specs=vmem(1)[0],
-        scratch_shapes=[
-            pltpu.VMEM((parts, slots * elems, 2 * LANES), bf16), ext, ext, picked, picked,
-            state, state, state, pltpu.VMEM((devices, LANES), jnp.int32),
-        ],
+        in_specs=[pl.BlockSpec(memory_space=pltpu.SMEM)] + vmem(4), out_specs=vmem(1)[0],
+        scratch_shapes=[ext, ext, picked, picked, state, state, state],
+        compiler_params=pltpu.CompilerParams(vmem_limit_bytes=24 << 20),
         name="solve",
-    )(scal, columns, w_hi, w_lo)
+    )(scal, columns, onehot, w_hi, w_lo)
     back = lax.all_to_all(done.reshape(parts, comps * pairs, LANES), "dom", split_axis=0, concat_axis=0, tiled=True)
     back = back.reshape(modes_dev, 2, comps, pairs, LANES).transpose(2, 0, 1, 3, 4)
     return back.reshape(comps, modes_dev, 2, merged)

time: 112 us -> 108 us (0.964)
  the two profiles are of different devices: /device:TPU:1 before, /device:TPU:32 now
where the time goes in v1:
time: 108 us; the launch traced here: 107 us
  blocking collectives  69.1 us (64%)
  Pallas kernels  20.8 us (19%)
  starting transfers between devices  11.5 us (11%)
  local copies, waits for them, and re-layouts  5.67 us (5%)
    all_to_all x1, blocking collectives, shards(): lax.all_to_all(both.transpose(1, 0, 2), 'mode', split_axis=0, concat_axis...  29.5 us
    all_to_all x1, blocking collectives, shards(): lax.all_to_all(done.reshape(parts, comps * pairs, LANES), 'dom', split_ax...  14.9 us
    pallas_call x1, Pallas kernels, shards(): pl.pallas_call(functools.partial(solve_kernel, parts, pairs, slots), out_...  14.6 us
    all_gather x1, blocking collectives, shards(): lax.all_gather(table, 'dom', axis=0, tiled=True, axis_index_groups=far)  12.4 us
    all_gather x1, blocking collectives, shards(): lax.all_gather(table, 'dom', axis=0, tiled=True, axis_index_groups=near)  12.3 us
    all_to_all x1, starting transfers between devices, shards(): lax.all_to_all(rhs, ('mode', 'dom'), split_axis=0, concat_axis=0, tiled=T...  11.5 us
    pallas_call x1, Pallas kernels, shards(): pl.pallas_call(functools.partial(prep_kernel, parts, pairs, slots, send),...  2.73 us
    unnamed x18, local copies, waits for them, and re-layouts  2.37 us
  transfers between devices with their start and end apart: 1, of which 0 were waited for; matrix products, arithmetic and copies ran while one was open for 0% of the time, Pallas kernels for 4%

profile of v1, /device:TPU:32, one launch (start us, length us, event | category | flops | bytes accessed | tf_op | source)
XLA Modules:
  0.0 107.4 jit_solution(8717870540795076294)
XLA Ops:
  0.0 0.0 copy-start.4
  0.0 1.4 %reshape.33 = f32[48,16,128]{2,1,0:T(8,128)S(1)} reshape(f32[3,8,2,2048]{3,2,1,0:T(2,128)} %param.7) | data formatting | bytes 786432 | tf_op jit(solution)/shard_map/reshape | solution.py:183
  1.4 0.1 copy.11
  1.5 0.0 copy-done.4
  1.5 0.3 reshape.34
  1.8 0.1 copy.12
  2.0 0.1 maximum_bitcast_fusion
  2.1 0.0 copy-start.2
  2.1 29.5 %all_to_all.15.lines = f32[16,96,128]{2,1,0:T(8,128)S(1)} all-to-all(f32[16,96,128]{2,1,0:T(8,128)S(1)} %maximum_bitcast_fusion), channel_id=1, replica_groups=mesh['mode'=16,'dom'=16] {'mode'}, dimensions={0} | all-to-all | bytes 1572864 | tf_op jit(solution)/shard_map/all_to_all | solution.py:184
  31.6 0.0 copy-done.2
  31.6 0.0 copy-start.6
  31.6 0.0 copy-start.5
  31.6 1.8 %lines.1 = f32[256,1,384]{2,1,0:T(1,128)} custom-call(f32[16,96,128]{2,1,0:T(8,128)S(1)} %all_to_all.15.lines, bf16[4,256,256]{2,1,0:T(8,128)(2,1)S(1)} %copy-done.2), custom_call_target="tpu_custom_call" | custom-call | tf_op jit(solution)/shard_map/lines/pallas_call | solution.py:208
  33.4 11.5 %all-to-all-start.1 = ((f32[256,1,384]{2,1,0:T(1,128)}), f32[256,1,384]{2,1,0:T(1,128)}, u32[]{:S(2)}, u32[]{:S(2)}) async-start(f32[256,1,384]{2,1,0:T(1,128)} %lines.1), calls=%async_computation.1 | async-start | bytes 786432 | tf_op jit(solution)/shard_map/all_to_all | solution.py:214
  44.9 0.0 copy-done.6
  44.9 0.1 reshape.42
  45.0 0.1 pad.6.clone
  45.1 0.0 copy-done.5
  45.1 0.1 copy.14
  45.2 0.1 reshape.38
  45.3 12.3 %all_gather.6 = f32[64,128]{1,0:T(8,128)S(1)} all-gather(f32[16,128]{1,0:T(8,128)S(1)} %pad.4), channel_id=1, replica_groups={{0,1,2,3},{4,5,6,7},{8,9,10,11},{12,13,14,15},{16,17,18,19},{20,21,22,2..., dimensions={0}, use_global_device_ids=true | all-gather | bytes 40960 | tf_op jit(solution)/shard_map/all_gather | solution.py:194
  57.6 12.4 %all_gather.7.table = f32[256,128]{1,0:T(8,128)S(1)} all-gather(f32[64,128]{1,0:T(8,128)S(1)} %all_gather.6), channel_id=1, replica_groups={{0,4,8,12},{1,5,9,13},{2,6,10,14},{3,7,11,15},{16,20,24,28},{17,21,25,2..., dimensions={0}, use_global_device_ids=true | all-gather | bytes 163840 | tf_op jit(solution)/shard_map/all_gather | solution.py:195
  70.0 0.0 copy-start.3
  70.0 0.0 copy-start.7
  70.0 2.7 %prep.1.onehot = bf16[16,288,256]{2,1,0:T(8,128)(2,1)S(1)} custom-call(f32[256,128]{1,0:T(8,128)S(1)} %all_gather.7.table), custom_call_target="tpu_custom_call" | custom-call | bytes 12582912 | tf_op jit(solution)/shard_map/prep/pallas_call | solution.py:196
  72.8 0.0 copy-done.3
  72.8 1.7 %weights.1 = (bf16[2304,256]{1,0:T(8,128)(2,1)S(1)}, bf16[2304,256]{1,0:T(8,128)(2,1)S(1)}) custom-call(f32[9,64,64]{2,1,0:T(8,128)S(1)} %copy-done.3), custom_call_target="tpu_custom_call" | custom-call | bytes 3145728 | tf_op jit(solution)/shard_map/weights/pallas_call | solution.py:216
  74.4 0.0 copy-start
  74.5 1.0 copy-done
  75.5 0.0 copy-done.7
  75.5 0.1 pad_maximum_fusion.scal
  75.5 0.0 all-to-all-done.1
  75.5 0.0 copy-start.1
  75.5 1.1 %copy.16 = f32[256,1,384]{2,0,1:T(8,128)S(1)} copy(f32[256,1,384]{2,1,0:T(1,128)} %all-to-all-done.1) | data formatting | bytes 786432
  76.7 0.1 copy.13
  76.8 0.1 copy-done.1
  76.9 14.6 %solve.1 = f32[16,3,16,128]{3,2,1,0:T(8,128)S(1)} custom-call(f32[9]{0:T(128)S(1)} %pad_maximum_fusion.scal, f32[256,384]{1,0:T(8,128)S(1)} %bitcast.17, bf16[16,288,256]{2,1,0:T(8,128)(2,1)S(1)} %prep.1.onehot, bf16[2304,256]{1,0:T(8,128)(2,1)S(1)} %get-tuple-element.7.w_hi, bf16[2304,256]{1,0:T(8,128)(2,1)S(1)} %copy-done.1), custom_call_target="tpu_custom_call" | custom-call | tf_op jit(solution)/shard_map/solve/pallas_call | solution.py:237
  91.5 14.9 %all_to_all.16 = f32[16,48,128]{2,1,0:T(8,128)S(1)} all-to-all(f32[16,48,128]{2,1,0:T(8,128)S(1)} %bitcast.18), channel_id=1, replica_groups=mesh['mode'=16,'dom'=16] {'dom'}, dimensions={0} | all-to-all | bytes 786432 | tf_op jit(solution)/shard_map/all_to_all | solution.py:245
  106.4 1.0 reshape.41
  (3 shorter events, 0.0 us)
Async XLA Ops:
  0.0 1.5 %copy-start.4 = (f32[3,8,2,2048]{3,2,1,0:T(2,128)S(1)}, f32[3,8,2,2048]{3,2,1,0:T(2,128)}, u32[]{:S(2)}) copy-start(f32[3,8,2,2048]{3,2,1,0:T(2,128)} %param.8) | copy-start | bytes 1179652
  2.1 29.5 %copy-start.2 = (bf16[4,256,256]{2,1,0:T(8,128)(2,1)S(1)}, bf16[4,256,256]{2,1,0:T(8,128)(2,1)}, u32[]{:S(2)}) copy-start(bf16[4,256,256]{2,1,0:T(8,128)(2,1)} %constant.38.clone.tables) | copy-start | bytes 1572868
  31.6 13.4 %copy-start.6 = (s32[2,8]{1,0:T(2,128)S(1)}, s32[2,8]{1,0:T(2,128)}, u32[]{:S(2)}) copy-start(s32[2,8]{1,0:T(2,128)} %param.11) | copy-start | bytes 196
  31.6 13.5 %copy-start.5 = (s32[9,32]{1,0:T(8,128)S(1)}, s32[9,32]{1,0:T(8,128)}, u32[]{:S(2)}) copy-start(s32[9,32]{1,0:T(8,128)} %param.10) | copy-start | bytes 3460
  33.4 42.2 %all-to-all-start.1 = ((f32[256,1,384]{2,1,0:T(1,128)}), f32[256,1,384]{2,1,0:T(1,128)}, u32[]{:S(2)}, u32[]{:S(2)}) async-start(f32[256,1,384]{2,1,0:T(1,128)} %lines.1), calls=%async_computation.1 | async-start | bytes 786432 | tf_op jit(solution)/shard_map/all_to_all | solution.py:214
  70.0 2.7 %copy-start.3 = (f32[9,64,64]{2,1,0:T(8,128)S(1)}, f32[9,64,64]{2,1,0:T(8,128)}, u32[]{:S(2)}) copy-start(f32[9,64,64]{2,1,0:T(8,128)} %blocks.1) | copy-start | bytes 442372
  70.0 5.5 %copy-start.7 = (f32[8]{0:T(128)S(1)}, f32[8]{0:T(128)}, u32[]{:S(2)}) copy-start(f32[8]{0:T(128)} %constant.39.clone) | copy-start | bytes 100
  74.4 1.0 copy-start
  75.5 1.4 %copy-start.1 = (bf16[2304,256]{1,0:T(8,128)(2,1)S(1)}, bf16[2304,256]{1,0:T(8,128)(2,1)}, u32[]{:S(2)}) copy-start(bf16[2304,256]{1,0:T(8,128)(2,1)} %copy-done) | copy-start | bytes 3538948

commit v2 on v1

v2 whole, which is shorter than its diff:
```python
import functools

import jax
import jax.numpy as jnp
import numpy as np
from jax import lax
from jax.experimental import pallas as pl
from jax.experimental.pallas import tpu as pltpu
from jax.sharding import PartitionSpec as P


CHEB = 4
NP = 64
COMPS = 3
LANES = 128
bf16, f32 = jnp.bfloat16, jnp.float32


def split(value):
    high = value.astype(bf16)
    return high, (value - high.astype(f32)).astype(bf16)


def np_split(value):
    high = value.astype(np.float32).astype(bf16)
    return high, (value - high.astype(np.float64)).astype(np.float32).astype(bf16)


def spanwise_tables(count):
    planes = 2 * count
    angle = 2 * np.pi / planes * ((np.arange(planes)[:, None] * np.arange(count)[None, :]) % planes)
    weights = np.where(np.arange(count) == 0, 1.0, 2.0)
    forward = np.stack([weights * np.cos(angle), -weights * np.sin(angle)], axis=2).reshape(planes, planes)
    back = np.stack([np.cos(angle).T, -np.sin(angle).T], axis=1).reshape(planes, planes) / planes
    return np.stack(np_split(forward) + np_split(back))


def dot(a, b):
    return jnp.dot(a, b, preferred_element_type=f32)


def dot3(a, b):
    return dot(a[0], b[0]) + dot(a[1], b[0]) + dot(a[0], b[1])


def lines_kernel(lines, tables, out):
    senders, rows, _ = lines.shape
    per = rows // (2 * COMPS)
    count = senders * per
    fields = [lines[:, i * per:(i + 1) * per, :].reshape(count, LANES) for i in range(2 * COMPS)]
    forward = (tables[0], tables[1])
    planes = [dot3(forward, split(jnp.concatenate(fields[i:i + 2], axis=1))) for i in range(0, 2 * COMPS, 2)]
    planes = [half for pair in planes for half in (pair[:, :LANES], pair[:, LANES:])]
    u, w = planes[:COMPS], planes[COMPS:]
    cross = jnp.concatenate([u[(c + 1) % 3] * w[(c + 2) % 3] - u[(c + 2) % 3] * w[(c + 1) % 3] for c in range(3)], axis=1)
    forcing = dot3((tables[2], tables[3]), split(cross))
    mode = lax.broadcasted_iota(jnp.int32, (count, LANES), 0) >> 1
    wavenum = mode.astype(f32) * (2.0 / count)
    inv_diag = 1.0 / (1.0 + 4.0 * wavenum * wavenum)
    for c in range(COMPS):
        out[:, 0, c * LANES:(c + 1) * LANES] = (fields[c] + forcing[:, c * LANES:(c + 1) * LANES]) * inv_diag


def prep_kernel(parts, pairs, slots, send, order, tables, blocks, onehot, weights, refs_at, kap):
    elems = 2 * pairs
    for k in range(parts):
        refs_at[pl.ds(pl.multiple_of(order[k] * pairs, pairs), pairs), :] = tables[k]

    refs = refs_at[...]
    below = jnp.concatenate([refs[-pairs:], refs[:-pairs]], axis=0)
    above = jnp.concatenate([refs[pairs:], refs[:pairs]], axis=0)
    local = refs
    first = 2 * slots
    for s in range(send):
        local = jnp.where(refs == float(elems + s), below[:, first + s:first + s + 1], local)
        at = first + send + s
        local = jnp.where(refs == float(elems + send + s), above[:, at:at + 1], local)
    local = local.astype(jnp.int32)
    place = jnp.where(refs < float(elems), elems, jnp.where(refs < float(elems + send), 0, 2 * elems))
    kap[...] = place + (local & 1) * pairs + (local >> 1)
    lane = lax.broadcasted_iota(jnp.int32, (pairs, LANES), 1)

    def build(d, carry):
        rows = kap[pl.ds(pl.multiple_of(d * pairs, pairs), pairs), :]
        for s in range(slots):
            for h in range(2):
                col = rows[:, h * slots + s:h * slots + s + 1]
                hit = jnp.where(lane == col, 1.0, 0.0).astype(bf16)
                onehot[d, s * elems + h * pairs:s * elems + (h + 1) * pairs, :] = hit
        return carry

    lax.fori_loop(0, parts, build, 0)

    weights[...] = jnp.zeros_like(weights)

    def place_block(s, carry):
        base = pl.multiple_of(s * LANES, LANES)
        for part, val in enumerate(split(blocks[s].T)):
            for c in range(2):
                at = part * LANES + c * NP
                weights[pl.ds(base + c * NP, NP), at:at + NP] = val
        return carry

    lax.fori_loop(0, slots, place_block, 0)


def solve_kernel(parts, pairs, slots, scal, state_in, onehot, weights, out,
                 ext_hi, ext_lo, picked, sol, resid, dirn):
    elems = 2 * pairs
    half = lax.broadcasted_iota(jnp.int32, (parts * pairs, LANES), 1) < NP
    x = [state_in[:, c * LANES:(c + 1) * LANES] for c in range(COMPS)]
    swap = [pltpu.roll(v, NP, 1) for v in x]
    shape = (parts, pairs, LANES)
    zero = jnp.zeros_like(x[0])
    dirn[0, :, 0] = jnp.where(half, x[0], swap[1]).reshape(shape)
    dirn[1, :, 0] = jnp.where(half, x[2], zero).reshape(shape)
    dirn[0, :, 1] = jnp.where(half, swap[0], x[1]).reshape(shape)
    dirn[1, :, 1] = jnp.where(half, swap[2], zero).reshape(shape)
    resid[...] = dirn[...]
    sol[...] = jnp.zeros_like(sol)
    inv_diag = scal[0]
    total_rows = parts * elems
    fill = jnp.zeros((LANES - 3 * elems, 2 * LANES), bf16)

    def step(i, carry):
        for j in range(2):
            lanes = slice(j * LANES, (j + 1) * LANES)
            for ext, val in zip((ext_hi, ext_lo), split(dirn[j].reshape(total_rows, LANES))):
                ext[elems:elems + total_rows, lanes] = val
                ext[:elems, lanes] = val[total_rows - elems:]
                ext[elems + total_rows:, lanes] = val[:elems]

        def gather(d, c):
            at = pl.ds(pl.multiple_of(d * elems, elems), 3 * elems)
            window = jnp.concatenate([ext_hi[at], fill, ext_lo[at], fill], axis=0)
            one = onehot[d]
            y = dot(jnp.concatenate([one, one], axis=1), window)
            to = pl.ds(pl.multiple_of(d * elems, elems), elems)
            for part, val in enumerate(split(y)):
                for s in range(slots):
                    at = (part * slots + s) * LANES
                    for j in range(2):
                        picked[j, to, at:at + LANES] = val[s * elems:(s + 1) * elems, j * LANES:(j + 1) * LANES]
            return c

        lax.fori_loop(0, parts, gather, 0, unroll=4)
        both = jnp.concatenate([weights[...], weights[...]], axis=0)
        total = dot(picked[...].reshape(2 * total_rows, 2 * slots * LANES), both)
        total = (total[:, :LANES] + total[:, LANES:]).reshape(dirn.shape)
        old = dirn[...]
        sol[...] = sol[...] + old
        left = resid[...] - (old + inv_diag * total)
        resid[...] = left
        dirn[...] = scal[1 + 2 * i] * old + scal[2 + 2 * i] * left
        return carry

    lax.fori_loop(0, CHEB, step, 0)
    final = sol[...] + dirn[...]
    a, b = [[final[j, :, h].reshape(parts * pairs, LANES) for h in range(2)] for j in range(2)]
    out[:, 0] = jnp.where(half, a[0], pltpu.roll(a[1], NP, 1)).reshape(shape)
    out[:, 1] = jnp.where(half, pltpu.roll(a[0], NP, 1), a[1]).reshape(shape)
    out[:, 2] = jnp.where(half, b[0], pltpu.roll(b[1], NP, 1)).reshape(shape)


def vmem(n):
    return [pl.BlockSpec(memory_space=pltpu.VMEM)] * n


def shards(velocity, vorticity, blocks, nbr_ref, send_list):
    comps, modes_dev, _, merged = velocity.shape
    n_mode, parts = lax.axis_size("mode"), lax.axis_size("dom")
    slots, elems = nbr_ref.shape
    send = send_list.shape[1]
    pairs = elems // 2
    modes_all = modes_dev * n_mode
    me = lax.axis_index("mode")
    rows = comps * modes_dev * 2

    both = jnp.concatenate([v.reshape(rows, n_mode, LANES) for v in (velocity, vorticity)], axis=0)
    lines = lax.all_to_all(both.transpose(1, 0, 2), "mode", split_axis=0, concat_axis=0, tiled=True)

    table = jnp.concatenate([
        nbr_ref.reshape(slots, pairs, 2).transpose(1, 2, 0).reshape(pairs, 2 * slots),
        jnp.broadcast_to(send_list.reshape(1, 2 * send), (pairs, 2 * send)),
    ], axis=1).astype(f32)
    table = jnp.pad(table, ((0, 0), (0, LANES - table.shape[1])))
    side = 4
    here = lax.axis_index("dom")
    near = [lax.ppermute(table, "dom", [(d, d // side * side + (d + i) % side) for d in range(parts)])
            for i in range(1, side)]
    table = jnp.stack([table] + near)
    far = [lax.ppermute(table, "dom", [(d, (d + i * side) % parts) for d in range(parts)])
           for i in range(1, parts // side)]
    table = jnp.concatenate([table] + far, axis=0)
    steps = jnp.arange(parts, dtype=jnp.int32)
    order = (here // side - steps // side) % (parts // side) * side + (here % side - steps % side) % side
    onehot, weights = pl.pallas_call(
        functools.partial(prep_kernel, parts, pairs, slots, send),
        out_shape=[jax.ShapeDtypeStruct((parts, slots * elems, LANES), bf16),
                   jax.ShapeDtypeStruct((slots * LANES, 2 * LANES), bf16)],
        in_specs=[pl.BlockSpec(memory_space=pltpu.SMEM)] + vmem(2), out_specs=vmem(2),
        scratch_shapes=[pltpu.VMEM((parts * pairs, LANES), f32), pltpu.VMEM((parts * pairs, LANES), jnp.int32)],
        compiler_params=pltpu.CompilerParams(vmem_limit_bytes=8 << 20),
        cost_estimate=pl.CostEstimate(flops=0, bytes_accessed=8 << 20, transcendentals=0),
        name="prep",
    )(order, table, blocks)

    width = comps * LANES
    devices = n_mode * parts
    rhs = pl.pallas_call(
        lines_kernel,
        out_shape=jax.ShapeDtypeStruct((devices, 1, width), f32),
        in_specs=vmem(2), out_specs=vmem(1)[0], name="lines",
        compiler_params=pltpu.CompilerParams(vmem_limit_bytes=12 << 20),
    )(lines, jnp.asarray(spanwise_tables(modes_all)))
    mode = me * modes_dev + lax.axis_index("dom") // 2
    wavenum = mode.astype(f32) / modes_all
    coefs = []
    rho = 0.5
    for _ in range(CHEB):
        rho_next = 1.0 / (4.0 - rho)
        coefs += [rho_next * rho, 4.0 * rho_next]
        rho = rho_next
    scal = jnp.concatenate([(1.0 / (1.0 + 4.0 * wavenum * wavenum)).reshape(1), jnp.asarray(coefs, f32)])
    rhs, scal, onehot, weights = lax.optimization_barrier((rhs, scal, onehot, weights))
    columns = lax.all_to_all(rhs, ("mode", "dom"), split_axis=0, concat_axis=0, tiled=True)
    columns = columns.reshape(n_mode, parts, width).transpose(1, 0, 2).reshape(devices, width)

    state = pltpu.VMEM((2, parts, 2, pairs, LANES), f32)
    ext = pltpu.VMEM(((parts + 2) * elems, 2 * LANES), bf16)
    picked = pltpu.VMEM((2, parts * elems, 2 * slots * LANES), bf16)
    done = pl.pallas_call(
        functools.partial(solve_kernel, parts, pairs, slots),
        out_shape=jax.ShapeDtypeStruct((parts, comps, pairs, LANES), f32),
        in_specs=[pl.BlockSpec(memory_space=pltpu.SMEM)] + vmem(3), out_specs=vmem(1)[0],
        scratch_shapes=[ext, ext, picked, state, state, state],
        compiler_params=pltpu.CompilerParams(vmem_limit_bytes=24 << 20),
        name="solve",
    )(scal, columns, onehot, weights)
    back = lax.all_to_all(done.reshape(parts, comps * pairs, LANES), "dom", split_axis=0, concat_axis=0, tiled=True)
    back = back.reshape(modes_dev, 2, comps, pairs, LANES).transpose(2, 0, 1, 3, 4)
    return back.reshape(comps, modes_dev, 2, merged)


def solution(mesh):
    placed = (
        P(None, "mode", None, "dom"),
        P(None, "mode", None, "dom"),
        P(),
        P(None, "dom"),
        P(None, "dom"),
    )
    return jax.shard_map(
        shards, mesh=mesh, in_specs=placed, out_specs=P(None, "mode", None, "dom"), check_vma=False
    )
```

time: 108 us -> 92.9 us (0.86)
  the two profiles are of different devices: /device:TPU:32 before, /device:TPU:1 now
where the time goes in v2:
time: 92.9 us; the launch traced here: 92.6 us
  blocking collectives  41.3 us (44%)
  starting transfers between devices  19.4 us (21%)
  Pallas kernels  19.3 us (21%)
  waiting for transfers between devices  7.95 us (9%)
  local copies, waits for them, and re-layouts  3.45 us (4%)
  other arithmetic  1.09 us (1%)
    all_to_all x1, blocking collectives, shards(): lax.all_to_all(rhs, ('mode', 'dom'), split_axis=0, concat_axis=0, tiled=T...  29.2 us
    pallas_call x1, Pallas kernels, shards(): pl.pallas_call(functools.partial(solve_kernel, parts, pairs, slots), out_...  13.3 us
    all_to_all x1, blocking collectives, shards(): lax.all_to_all(done.reshape(parts, comps * pairs, LANES), 'dom', split_ax...  12.1 us
    all_to_all x1, starting transfers between devices, shards(): lax.all_to_all(both.transpose(1, 0, 2), 'mode', split_axis=0, concat_axis...  10.1 us
    ppermute x3, starting transfers between devices, shards(): lax.ppermute(table, 'dom', [(d, d // side * side + (d + i) % side) for d...  5.5 us
    pallas_call x1, Pallas kernels, shards(): pl.pallas_call(functools.partial(prep_kernel, parts, pairs, slots, send),...  4.91 us
    ppermute x3, waiting for transfers between devices, shards(): lax.ppermute(table, 'dom', [(d, (d + i * side) % parts) for d in range(pa...  3.87 us
    ppermute x3, starting transfers between devices, shards(): lax.ppermute(table, 'dom', [(d, (d + i * side) % parts) for d in range(pa...  3.78 us
  transfers between devices with their start and end apart: 7, of which 3 were waited for; matrix products, arithmetic and copies ran while one was open for 0% of the time, Pallas kernels for 5%

profile of v2, /device:TPU:1, one launch (start us, length us, event | category | flops | bytes accessed | tf_op | source)
XLA Modules:
  0.0 92.6 jit_solution(11729567635804383366)
XLA Ops:
  0.0 0.0 copy-start.2
  0.0 1.4 %reshape.32 = f32[48,16,128]{2,1,0:T(8,128)S(1)} reshape(f32[3,8,2,2048]{3,2,1,0:T(2,128)} %param.7) | data formatting | bytes 786432 | tf_op jit(solution)/shard_map/reshape | solution.py:179
  1.4 0.1 copy.11
  1.5 0.0 copy-done.2
  1.5 0.3 reshape.33
  1.8 0.1 copy.12
  2.0 0.0 copy-start.4
  2.0 1.0 %maximum_bitcast_fusion = f32[16,96,128]{2,1,0:T(8,128)} fusion(f32[48,16,128]{2,0,1:T(8,128)S(1)} %copy.12, f32[48,16,128]{2,0,1:T(8,128)S(1)} %copy.11), kind=kLoop, calls=%fused_computation | loop fusion | flops 196608 | bytes 1572864 | tf_op jit(solution)/shard_map/transpose | solution.py:180
  3.0 0.0 copy-start.3
  3.0 0.0 copy-start.5
  3.0 0.0 copy-start.1
  3.0 0.0 copy-start
  3.0 10.1 %all-to-all-start = ((f32[16,96,128]{2,1,0:T(8,128)}), f32[16,96,128]{2,1,0:T(8,128)S(1)}, u32[]{:S(2)}, u32[]{:S(2)}) async-start(f32[16,96,128]{2,1,0:T(8,128)} %maximum_bitcast_fusion), calls=%async_computation | async-start | bytes 1572864 | tf_op jit(solution)/shard_map/all_to_all | solution.py:180
  13.1 0.0 copy-done.4
  13.1 0.1 reshape.42
  13.2 0.0 copy-done.3
  13.2 0.1 copy.13
  13.3 0.1 reshape.36
  13.4 0.1 pad.10.clone
  13.5 2.8 %collective-permute-start.1 = (f32[16,128]{1,0:T(8,128)S(1)}, f32[16,128]{1,0:T(8,128)S(1)}, u32[]{:S(2)}, u32[]{:S(2)}) collective-permute-start(f32[16,128]{1,0:T(8,128)S(1)} %get-tuple-element.18), channel_id=1, source_target_pairs={{0,2},{1,3},{2,0},{3,1},{4,6},{5,7},{6,4},{7,5},{8,10},{9,11},{10,... | collective-permute-start | bytes 24584 | tf_op jit(solution)/shard_map/ppermute | solution.py:189
  16.3 0.3 collective-permute-start
  16.6 2.4 %collective-permute-start.2 = (f32[16,128]{1,0:T(8,128)S(1)}, f32[16,128]{1,0:T(8,128)S(1)}, u32[]{:S(2)}, u32[]{:S(2)}) collective-permute-start(f32[16,128]{1,0:T(8,128)S(1)} %get-tuple-element.18), channel_id=1, source_target_pairs={{0,3},{1,0},{2,1},{3,2},{4,7},{5,4},{6,5},{7,6},{8,11},{9,8},{10,9... | collective-permute-start | bytes 24584 | tf_op jit(solution)/shard_map/ppermute | solution.py:189
  19.0 0.0 copy-done.5
  19.0 0.1 pad_maximum_fusion.1.scal
  19.1 0.0 collective-permute-done.1
  19.1 1.2 %collective-permute-done = f32[16,128]{1,0:T(8,128)S(1)} collective-permute-done((f32[16,128]{1,0:T(8,128)S(1)}, f32[16,128]{1,0:T(8,128)S(1)}, u32[]{:S(2)}, u32[]{:S(2)}) %collective-permute-start) | collective-permute-done | bytes 8224 | tf_op jit(solution)/shard_map/ppermute | solution.py:189
  20.3 0.0 collective-permute-done.2
  20.3 2.7 %collective-permute-start.5 = (f32[4,16,128]{2,1,0:T(8,128)S(1)}, f32[4,16,128]{2,1,0:T(8,128)S(1)}, u32[]{:S(2)}, u32[]{:S(2)}) collective-permute-start(f32[4,16,128]{2,1,0:T(8,128)S(1)} %pad_maximum_fusion), channel_id=1, source_target_pairs={{0,12},{1,13},{2,14},{3,15},{4,0},{5,1},{6,2},{7,3},{8,4},{9,5},{1... | collective-permute-start | bytes 98312 | tf_op jit(solution)/shard_map/ppermute | solution.py:192
  23.0 0.3 collective-permute-start.4
  23.4 0.7 collective-permute-start.3
  24.1 3.9 %collective-permute-done.3 = f32[4,16,128]{2,1,0:T(8,128)S(1)} collective-permute-done((f32[4,16,128]{2,1,0:T(8,128)S(1)}, f32[4,16,128]{2,1,0:T(8,128)S(1)}, u32[]{:S(2)}, u32[]{:S(2)}) %collective-permute-start.3) | collective-permute-done | bytes 32800 | tf_op jit(solution)/shard_map/ppermute | solution.py:192
  27.9 0.0 collective-permute-done.4
  28.0 0.0 collective-permute-done.5
  28.0 0.0 copy-done.1
  28.0 4.9 %prep.1 = (bf16[16,288,128]{2,1,0:T(8,128)(2,1)S(1)}, bf16[1152,256]{1,0:T(8,128)(2,1)S(1)}) custom-call(s32[16]{0:T(128)S(1)} %fusion.1.order, f32[16,16,128]{2,1,0:T(8,128)S(1)} %constant_dynamic-update-slice_fusion.tables, f32[9,64,64]{2,1,0:T(8,128)S(1)} %copy-done.1), custom_call_target="tpu_custom_call" | custom-call | bytes 8388608 | tf_op jit(solution)/shard_map/prep/pallas_call | solution.py:197
  32.9 2.9 %all-to-all-done.lines = f32[16,96,128]{2,1,0:T(8,128)S(1)} async-done(((f32[16,96,128]{2,1,0:T(8,128)}), f32[16,96,128]{2,1,0:T(8,128)S(1)}, u32[]{:S(2)}, u32[]{:S(2)}) %all-to-all-start) | async-done | bytes 786464 | tf_op jit(solution)/shard_map/all_to_all | solution.py:180
  35.8 0.0 copy-done
  35.8 1.1 %lines.1 = f32[256,1,384]{2,1,0:T(1,128)S(1)} custom-call(f32[16,96,128]{2,1,0:T(8,128)S(1)} %all-to-all-done.lines, bf16[4,256,256]{2,1,0:T(8,128)(2,1)S(1)} %copy-done), custom_call_target="tpu_custom_call" | custom-call | tf_op jit(solution)/shard_map/lines/pallas_call | solution.py:210
  36.9 29.2 %all_to_all.15 = f32[256,1,384]{2,1,0:T(1,128)S(1)} all-to-all(f32[256,1,384]{2,1,0:T(1,128)S(1)} %lines.1), channel_id=1, replica_groups=mesh['mode'=16,'dom'=16] {'mode','dom'}, dimensions={0} | all-to-all | bytes 786432 | tf_op jit(solution)/shard_map/all_to_all | solution.py:226
  66.1 0.1 copy.14
  66.2 13.3 %solve.1 = f32[16,3,16,128]{3,2,1,0:T(8,128)S(1)} custom-call(f32[9]{0:T(128)S(1)} %pad_maximum_fusion.1.scal, f32[256,384]{1,0:T(8,128)S(1)} %bitcast.26, bf16[16,288,128]{2,1,0:T(8,128)(2,1)S(1)} %get-tuple-element.15.onehot, bf16[1152,256]{1,0:T(8,128)(2,1)S(1)} %get-tuple-element.16.weights), custom_call_target="tpu_custom_call" | custom-call | tf_op jit(solution)/shard_map/solve/pallas_call | solution.py:232
  79.5 12.1 %all_to_all.16 = f32[16,48,128]{2,1,0:T(8,128)S(1)} all-to-all(f32[16,48,128]{2,1,0:T(8,128)S(1)} %bitcast.27), channel_id=1, replica_groups=mesh['mode'=16,'dom'=16] {'dom'}, dimensions={0} | all-to-all | bytes 786432 | tf_op jit(solution)/shard_map/all_to_all | solution.py:240
  91.7 1.0 %reshape.41 = f32[3,8,2,2048]{3,2,1,0:T(2,128)} reshape(f32[3,8,2,16,128]{4,3,2,1,0:T(8,128)S(1)} %bitcast.30) | data formatting | bytes 786432 | tf_op jit(solution)/shard_map/reshape | solution.py:242
  (13 shorter events, 0.1 us)
Async XLA Ops:
  0.0 1.5 %copy-start.2 = (f32[3,8,2,2048]{3,2,1,0:T(2,128)S(1)}, f32[3,8,2,2048]{3,2,1,0:T(2,128)}, u32[]{:S(2)}) copy-start(f32[3,8,2,2048]{3,2,1,0:T(2,128)} %param.8) | copy-start | bytes 1179652
  2.0 11.1 %copy-start.4 = (s32[2,8]{1,0:T(2,128)S(1)}, s32[2,8]{1,0:T(2,128)}, u32[]{:S(2)}) copy-start(s32[2,8]{1,0:T(2,128)} %param.11) | copy-start | bytes 196
  3.0 10.2 %copy-start.3 = (s32[9,32]{1,0:T(8,128)S(1)}, s32[9,32]{1,0:T(8,128)}, u32[]{:S(2)}) copy-start(s32[9,32]{1,0:T(8,128)} %param.10) | copy-start | bytes 3460
  3.0 16.1 %copy-start.5 = (f32[8]{0:T(128)S(1)}, f32[8]{0:T(128)}, u32[]{:S(2)}) copy-start(f32[8]{0:T(128)} %constant.91.clone) | copy-start | bytes 100
  3.0 25.0 %copy-start.1 = (f32[9,64,64]{2,1,0:T(8,128)S(1)}, f32[9,64,64]{2,1,0:T(8,128)}, u32[]{:S(2)}) copy-start(f32[9,64,64]{2,1,0:T(8,128)} %blocks.1) | copy-start | bytes 442372
  3.0 32.8 %copy-start = (bf16[4,256,256]{2,1,0:T(8,128)(2,1)S(1)}, bf16[4,256,256]{2,1,0:T(8,128)(2,1)}, u32[]{:S(2)}) copy-start(bf16[4,256,256]{2,1,0:T(8,128)(2,1)} %constant.90.clone.tables) | copy-start | bytes 1572868
  3.0 32.8 %all-to-all-start = ((f32[16,96,128]{2,1,0:T(8,128)}), f32[16,96,128]{2,1,0:T(8,128)S(1)}, u32[]{:S(2)}, u32[]{:S(2)}) async-start(f32[16,96,128]{2,1,0:T(8,128)} %maximum_bitcast_fusion), calls=%async_computation | async-start | bytes 1572864 | tf_op jit(solution)/shard_map/all_to_all | solution.py:180
  13.5 5.7 %collective-permute-start.1 = (f32[16,128]{1,0:T(8,128)S(1)}, f32[16,128]{1,0:T(8,128)S(1)}, u32[]{:S(2)}, u32[]{:S(2)}) collective-permute-start(f32[16,128]{1,0:T(8,128)S(1)} %get-tuple-element.18), channel_id=1, source_target_pairs={{0,2},{1,3},{2,0},{3,1},{4,6},{5,7},{6,4},{7,5},{8,10},{9,11},{10,... | collective-permute-start | bytes 24584 | tf_op jit(solution)/shard_map/ppermute | solution.py:189
  16.3 4.0 %collective-permute-start = (f32[16,128]{1,0:T(8,128)S(1)}, f32[16,128]{1,0:T(8,128)S(1)}, u32[]{:S(2)}, u32[]{:S(2)}) collective-permute-start(f32[16,128]{1,0:T(8,128)S(1)} %get-tuple-element.18), channel_id=1, source_target_pairs={{0,1},{1,2},{2,3},{3,0},{4,5},{5,6},{6,7},{7,4},{8,9},{9,10},{10,1... | collective-permute-start | bytes 24584 | tf_op jit(solution)/shard_map/ppermute | solution.py:189
  16.6 3.7 %collective-permute-start.2 = (f32[16,128]{1,0:T(8,128)S(1)}, f32[16,128]{1,0:T(8,128)S(1)}, u32[]{:S(2)}, u32[]{:S(2)}) collective-permute-start(f32[16,128]{1,0:T(8,128)S(1)} %get-tuple-element.18), channel_id=1, source_target_pairs={{0,3},{1,0},{2,1},{3,2},{4,7},{5,4},{6,5},{7,6},{8,11},{9,8},{10,9... | collective-permute-start | bytes 24584 | tf_op jit(solution)/shard_map/ppermute | solution.py:189
  20.3 7.7 %collective-permute-start.5 = (f32[4,16,128]{2,1,0:T(8,128)S(1)}, f32[4,16,128]{2,1,0:T(8,128)S(1)}, u32[]{:S(2)}, u32[]{:S(2)}) collective-permute-start(f32[4,16,128]{2,1,0:T(8,128)S(1)} %pad_maximum_fusion), channel_id=1, source_target_pairs={{0,12},{1,13},{2,14},{3,15},{4,0},{5,1},{6,2},{7,3},{8,4},{9,5},{1... | collective-permute-start | bytes 98312 | tf_op jit(solution)/shard_map/ppermute | solution.py:192
  23.0 4.9 %collective-permute-start.4 = (f32[4,16,128]{2,1,0:T(8,128)S(1)}, f32[4,16,128]{2,1,0:T(8,128)S(1)}, u32[]{:S(2)}, u32[]{:S(2)}) collective-permute-start(f32[4,16,128]{2,1,0:T(8,128)S(1)} %pad_maximum_fusion), channel_id=1, source_target_pairs={{0,8},{1,9},{2,10},{3,11},{4,12},{5,13},{6,14},{7,15},{8,0},{9,1},... | collective-permute-start | bytes 98312 | tf_op jit(solution)/shard_map/ppermute | solution.py:192
  23.4 4.6 %collective-permute-start.3 = (f32[4,16,128]{2,1,0:T(8,128)S(1)}, f32[4,16,128]{2,1,0:T(8,128)S(1)}, u32[]{:S(2)}, u32[]{:S(2)}) collective-permute-start(f32[4,16,128]{2,1,0:T(8,128)S(1)} %pad_maximum_fusion), channel_id=1, source_target_pairs={{0,4},{1,5},{2,6},{3,7},{4,8},{5,9},{6,10},{7,11},{8,12},{9,13},{1... | collective-permute-start | bytes 98312 | tf_op jit(solution)/shard_map/ppermute | solution.py:192

commit v3 on v2

--- a/solution.py
+++ b/solution.py
@@ -10,6 +10,7 @@
 
 
 CHEB = 4
+UNROLL = 4
 NP = 64
 COMPS = 3
 LANES = 128
@@ -61,23 +62,31 @@
         out[:, 0, c * LANES:(c + 1) * LANES] = (fields[c] + forcing[:, c * LANES:(c + 1) * LANES]) * inv_diag
 
 
+def first_send(slots):
+    return -(-2 * slots // 8) * 8
+
+
 def prep_kernel(parts, pairs, slots, send, order, tables, blocks, onehot, weights, refs_at, kap):
     elems = 2 * pairs
     for k in range(parts):
         refs_at[pl.ds(pl.multiple_of(order[k] * pairs, pairs), pairs), :] = tables[k]
 
-    refs = refs_at[...]
-    below = jnp.concatenate([refs[-pairs:], refs[:-pairs]], axis=0)
-    above = jnp.concatenate([refs[pairs:], refs[:pairs]], axis=0)
+    turned = refs_at[...].T
+    first = first_send(slots)
+    refs = turned[:first]
+    shared = turned[first:first + 2 * send]
+    below = pltpu.roll(shared, pairs, 1)
+    above = pltpu.roll(shared, (parts - 1) * pairs, 1)
     local = refs
-    first = 2 * slots
     for s in range(send):
-        local = jnp.where(refs == float(elems + s), below[:, first + s:first + s + 1], local)
-        at = first + send + s
-        local = jnp.where(refs == float(elems + send + s), above[:, at:at + 1], local)
+        local = jnp.where(refs == float(elems + s), below[s:s + 1], local)
+        local = jnp.where(refs == float(elems + send + s), above[send + s:send + s + 1], local)
     local = local.astype(jnp.int32)
     place = jnp.where(refs < float(elems), elems, jnp.where(refs < float(elems + send), 0, 2 * elems))
-    kap[...] = place + (local & 1) * pairs + (local >> 1)
+    odd = (lax.broadcasted_iota(jnp.int32, place.shape, 1) // pairs) & 1
+    place = (place + odd * elems + (local & 1) * pairs + (local >> 1)).astype(f32)
+    place = jnp.concatenate([place, jnp.zeros((LANES - first, parts * pairs), f32)], axis=0)
+    kap[...] = place.T.astype(jnp.int32)
     lane = lax.broadcasted_iota(jnp.int32, (pairs, LANES), 1)
 
     def build(d, carry):
@@ -86,10 +95,11 @@
             for h in range(2):
                 col = rows[:, h * slots + s:h * slots + s + 1]
                 hit = jnp.where(lane == col, 1.0, 0.0).astype(bf16)
-                onehot[d, s * elems + h * pairs:s * elems + (h + 1) * pairs, :] = hit
+                at = pl.multiple_of((d & 1) * slots * elems, elems) + s * elems + h * pairs
+                onehot[d >> 1, pl.ds(at, pairs), :] = hit
         return carry
 
-    lax.fori_loop(0, parts, build, 0)
+    lax.fori_loop(0, parts, build, 0, unroll=4)
 
     weights[...] = jnp.zeros_like(weights)
 
@@ -101,52 +111,59 @@
                 weights[pl.ds(base + c * NP, NP), at:at + NP] = val
         return carry
 
-    lax.fori_loop(0, slots, place_block, 0)
+    lax.fori_loop(0, slots, place_block, 0, unroll=3)
 
 
 def solve_kernel(parts, pairs, slots, scal, state_in, onehot, weights, out,
-                 ext_hi, ext_lo, picked, sol, resid, dirn):
+                 ext, picked, sol, resid, dirn):
     elems = 2 * pairs
-    half = lax.broadcasted_iota(jnp.int32, (parts * pairs, LANES), 1) < NP
+    ones, twos = parts * pairs, parts * elems
+    half = lax.broadcasted_iota(jnp.int32, (ones, LANES), 1) < NP
+    few = half[:pairs]
     x = [state_in[:, c * LANES:(c + 1) * LANES] for c in range(COMPS)]
-    swap = [pltpu.roll(v, NP, 1) for v in x]
     shape = (parts, pairs, LANES)
-    zero = jnp.zeros_like(x[0])
-    dirn[0, :, 0] = jnp.where(half, x[0], swap[1]).reshape(shape)
-    dirn[1, :, 0] = jnp.where(half, x[2], zero).reshape(shape)
-    dirn[0, :, 1] = jnp.where(half, swap[0], x[1]).reshape(shape)
-    dirn[1, :, 1] = jnp.where(half, swap[2], zero).reshape(shape)
+
+    def halves(low, high):
+        return jnp.stack([low.reshape(shape), high.reshape(shape)], axis=1).reshape(twos, LANES)
+
+    dirn[:twos] = halves(jnp.where(half, x[0], pltpu.roll(x[1], NP, 1)), jnp.where(half, pltpu.roll(x[0], NP, 1), x[1]))
+    dirn[twos:] = x[2]
     resid[...] = dirn[...]
     sol[...] = jnp.zeros_like(sol)
     inv_diag = scal[0]
-    total_rows = parts * elems
-    fill = jnp.zeros((LANES - 3 * elems, 2 * LANES), bf16)
 
     def step(i, carry):
-        for j in range(2):
-            lanes = slice(j * LANES, (j + 1) * LANES)
-            for ext, val in zip((ext_hi, ext_lo), split(dirn[j].reshape(total_rows, LANES))):
-                ext[elems:elems + total_rows, lanes] = val
-                ext[:elems, lanes] = val[total_rows - elems:]
-                ext[elems + total_rows:, lanes] = val[:elems]
-
-        def gather(d, c):
-            at = pl.ds(pl.multiple_of(d * elems, elems), 3 * elems)
-            window = jnp.concatenate([ext_hi[at], fill, ext_lo[at], fill], axis=0)
-            one = onehot[d]
+        last = dirn[twos:]
+        turned = pltpu.roll(last, NP, 1)
+        for j, now in enumerate((dirn[:twos], halves(jnp.where(half, last, turned), jnp.where(half, turned, last)))):
+            for part, val in enumerate(split(now)):
+                lanes = slice((2 * part + j) * LANES, (2 * part + j + 1) * LANES)
+                ext[elems:elems + twos, lanes] = val
+                ext[:elems, lanes] = val[twos - elems:]
+                ext[elems + twos:, lanes] = val[:elems]
+
+        def gather(g, c):
+            near = ext[pl.ds(pl.multiple_of(g * 2 * elems, 2 * elems), 4 * elems)]
+            window = jnp.concatenate([near[:, :2 * LANES], near[:, 2 * LANES:]], axis=0)
+            one = onehot[g]
             y = dot(jnp.concatenate([one, one], axis=1), window)
-            to = pl.ds(pl.multiple_of(d * elems, elems), elems)
-            for part, val in enumerate(split(y)):
+            for k in range(2):
+                two = pl.ds(pl.multiple_of((2 * g + k) * elems, elems), elems)
+                single = pl.ds(pl.multiple_of(twos + (2 * g + k) * pairs, pairs), pairs)
                 for s in range(slots):
-                    at = (part * slots + s) * LANES
-                    for j in range(2):
-                        picked[j, to, at:at + LANES] = val[s * elems:(s + 1) * elems, j * LANES:(j + 1) * LANES]
+                    row = (k * slots + s) * elems
+                    both = y[row:row + elems, :LANES]
+                    last = y[row:row + elems, LANES:]
+                    last = jnp.where(few, last[:pairs], last[pairs:])
+                    for at, val in ((two, both), (single, last)):
+                        for part, piece in enumerate(split(val)):
+                            at_lane = (part * slots + s) * LANES
+                            picked[at, at_lane:at_lane + LANES] = piece
             return c
 
-        lax.fori_loop(0, parts, gather, 0, unroll=4)
-        both = jnp.concatenate([weights[...], weights[...]], axis=0)
-        total = dot(picked[...].reshape(2 * total_rows, 2 * slots * LANES), both)
-        total = (total[:, :LANES] + total[:, LANES:]).reshape(dirn.shape)
+        lax.fori_loop(0, parts // 2, gather, 0, unroll=UNROLL)
+        total = dot(picked[...], jnp.concatenate([weights[...], weights[...]], axis=0))
+        total = total[:, :LANES] + total[:, LANES:]
         old = dirn[...]
         sol[...] = sol[...] + old
         left = resid[...] - (old + inv_diag * total)
@@ -156,10 +173,11 @@
 
     lax.fori_loop(0, CHEB, step, 0)
     final = sol[...] + dirn[...]
-    a, b = [[final[j, :, h].reshape(parts * pairs, LANES) for h in range(2)] for j in range(2)]
+    both = final[:twos].reshape(parts, 2, pairs, LANES)
+    a = [both[:, h].reshape(ones, LANES) for h in range(2)]
     out[:, 0] = jnp.where(half, a[0], pltpu.roll(a[1], NP, 1)).reshape(shape)
     out[:, 1] = jnp.where(half, pltpu.roll(a[0], NP, 1), a[1]).reshape(shape)
-    out[:, 2] = jnp.where(half, b[0], pltpu.roll(b[1], NP, 1)).reshape(shape)
+    out[:, 2] = final[twos:].reshape(shape)
 
 
 def vmem(n):
@@ -181,6 +199,7 @@
 
     table = jnp.concatenate([
         nbr_ref.reshape(slots, pairs, 2).transpose(1, 2, 0).reshape(pairs, 2 * slots),
+        jnp.zeros((pairs, first_send(slots) - 2 * slots), jnp.int32),
         jnp.broadcast_to(send_list.reshape(1, 2 * send), (pairs, 2 * send)),
     ], axis=1).astype(f32)
     table = jnp.pad(table, ((0, 0), (0, LANES - table.shape[1])))
@@ -196,7 +215,7 @@
     order = (here // side - steps // side) % (parts // side) * side + (here % side - steps % side) % side
     onehot, weights = pl.pallas_call(
         functools.partial(prep_kernel, parts, pairs, slots, send),
-        out_shape=[jax.ShapeDtypeStruct((parts, slots * elems, LANES), bf16),
+        out_shape=[jax.ShapeDtypeStruct((parts // 2, 2 * slots * elems, LANES), bf16),
                    jax.ShapeDtypeStruct((slots * LANES, 2 * LANES), bf16)],
         in_specs=[pl.BlockSpec(memory_space=pltpu.SMEM)] + vmem(2), out_specs=vmem(2),
         scratch_shapes=[pltpu.VMEM((parts * pairs, LANES), f32), pltpu.VMEM((parts * pairs, LANES), jnp.int32)],
@@ -226,14 +245,15 @@
     columns = lax.all_to_all(rhs, ("mode", "dom"), split_axis=0, concat_axis=0, tiled=True)
     columns = columns.reshape(n_mode, parts, width).transpose(1, 0, 2).reshape(devices, width)
 
-    state = pltpu.VMEM((2, parts, 2, pairs, LANES), f32)
-    ext = pltpu.VMEM(((parts + 2) * elems, 2 * LANES), bf16)
-    picked = pltpu.VMEM((2, parts * elems, 2 * slots * LANES), bf16)
+    rows = parts * pairs * 3
+    state = pltpu.VMEM((rows, LANES), f32)
+    ext = pltpu.VMEM(((parts + 2) * elems, 4 * LANES), bf16)
+    picked = pltpu.VMEM((rows, 2 * slots * LANES), bf16)
     done = pl.pallas_call(
         functools.partial(solve_kernel, parts, pairs, slots),
         out_shape=jax.ShapeDtypeStruct((parts, comps, pairs, LANES), f32),
         in_specs=[pl.BlockSpec(memory_space=pltpu.SMEM)] + vmem(3), out_specs=vmem(1)[0],
-        scratch_shapes=[ext, ext, picked, state, state, state],
+        scratch_shapes=[ext, picked, state, state, state],
         compiler_params=pltpu.CompilerParams(vmem_limit_bytes=24 << 20),
         name="solve",
     )(scal, columns, onehot, weights)

time: 92.9 us -> 88 us (0.947)
  Pallas kernels: 19.3 us -> 14.3 us
  blocking collectives: 41.3 us -> 39.1 us
  waiting for transfers between devices: 7.95 us -> 10.1 us
    pallas_call x1, Pallas kernels: 13.3 us -> 10.5 us  [shards(): pl.pallas_call(functools.partial(solve_kernel, parts, pairs, slots), out_...]
    pallas_call x1, Pallas kernels: 4.91 us -> 2.71 us  [shards(): pl.pallas_call(functools.partial(prep_kernel, parts, pairs, slots, send),...]
    all_to_all x1, waiting for transfers between devices: 2.91 us -> 5.03 us  [shards(): lax.all_to_all(both.transpose(1, 0, 2), 'mode', split_axis=0, concat_axis...]
    all_to_all x1, blocking collectives: 29.2 us -> 27.1 us  [shards(): lax.all_to_all(rhs, ('mode', 'dom'), split_axis=0, concat_axis=0, tiled=T...]
  transfers between devices with their start and end apart: 7 -> 7, of which waited for: 3 -> 3; matrix products, arithmetic and copies ran while one was open for 0% -> 1% of each run, Pallas kernels for 5% -> 3%
where the time goes in v3:
time: 88 us; the launch traced here: 87.7 us
  blocking collectives  39.1 us (44%)
  starting transfers between devices  19.4 us (22%)
  Pallas kernels  14.3 us (16%)
  waiting for transfers between devices  10.1 us (11%)
  local copies, waits for them, and re-layouts  3.53 us (4%)
  other arithmetic  1.09 us (1%)
    all_to_all x1, blocking collectives, shards(): lax.all_to_all(rhs, ('mode', 'dom'), split_axis=0, concat_axis=0, tiled=T...  27.1 us
    all_to_all x1, blocking collectives, shards(): lax.all_to_all(done.reshape(parts, comps * pairs, LANES), 'dom', split_ax...  12.1 us
    pallas_call x1, Pallas kernels, shards(): pl.pallas_call(functools.partial(solve_kernel, parts, pairs, slots), out_...  10.5 us
    all_to_all x1, starting transfers between devices, shards(): lax.all_to_all(both.transpose(1, 0, 2), 'mode', split_axis=0, concat_axis...  10.1 us
    ppermute x3, starting transfers between devices, shards(): lax.ppermute(table, 'dom', [(d, d // side * side + (d + i) % side) for d...  5.51 us
    all_to_all x1, waiting for transfers between devices, shards(): lax.all_to_all(both.transpose(1, 0, 2), 'mode', split_axis=0, concat_axis...  5.03 us
    ppermute x3, waiting for transfers between devices, shards(): lax.ppermute(table, 'dom', [(d, (d + i * side) % parts) for d in range(pa...  3.87 us
    ppermute x3, starting transfers between devices, shards(): lax.ppermute(table, 'dom', [(d, (d + i * side) % parts) for d in range(pa...  3.78 us
  transfers between devices with their start and end apart: 7, of which 3 were waited for; matrix products, arithmetic and copies ran while one was open for 1% of the time, Pallas kernels for 3%

profile of v3, /device:TPU:1, one launch (start us, length us, event | category | flops | bytes accessed | tf_op | source)
XLA Modules:
  0.0 87.7 jit_solution(15297107642980549271)
XLA Ops:
  0.0 0.0 copy-start.2
  0.0 1.4 %reshape.32 = f32[48,16,128]{2,1,0:T(8,128)S(1)} reshape(f32[3,8,2,2048]{3,2,1,0:T(2,128)} %param.7) | data formatting | bytes 786432 | tf_op jit(solution)/shard_map/reshape | solution.py:197
  1.4 0.1 copy.11
  1.5 0.0 copy-done.2
  1.5 0.3 reshape.33
  1.8 0.1 copy.12
  2.0 0.0 copy-start.4
  2.0 1.0 %maximum_bitcast_fusion = f32[16,96,128]{2,1,0:T(8,128)} fusion(f32[48,16,128]{2,0,1:T(8,128)S(1)} %copy.12, f32[48,16,128]{2,0,1:T(8,128)S(1)} %copy.11), kind=kLoop, calls=%fused_computation | loop fusion | flops 196608 | bytes 1572864 | tf_op jit(solution)/shard_map/transpose | solution.py:198
  3.0 0.0 copy-start.3
  3.0 0.0 copy-start.5
  3.0 0.0 copy-start.1
  3.0 0.0 copy-start
  3.0 10.1 %all-to-all-start = ((f32[16,96,128]{2,1,0:T(8,128)}), f32[16,96,128]{2,1,0:T(8,128)S(1)}, u32[]{:S(2)}, u32[]{:S(2)}) async-start(f32[16,96,128]{2,1,0:T(8,128)} %maximum_bitcast_fusion), calls=%async_computation | async-start | bytes 1572864 | tf_op jit(solution)/shard_map/all_to_all | solution.py:198
  13.1 0.0 copy-done.4
  13.1 0.1 reshape.42
  13.2 0.1 pad.11.clone
  13.3 0.1 pad.10.clone
  13.3 0.0 copy-done.3
  13.3 0.1 copy.13
  13.4 0.1 reshape.36
  13.5 2.8 %collective-permute-start.1 = (f32[16,128]{1,0:T(8,128)S(1)}, f32[16,128]{1,0:T(8,128)S(1)}, u32[]{:S(2)}, u32[]{:S(2)}) collective-permute-start(f32[16,128]{1,0:T(8,128)S(1)} %get-tuple-element.18), channel_id=1, source_target_pairs={{0,2},{1,3},{2,0},{3,1},{4,6},{5,7},{6,4},{7,5},{8,10},{9,11},{10,... | collective-permute-start | bytes 24584 | tf_op jit(solution)/shard_map/ppermute | solution.py:208
  16.4 0.3 collective-permute-start
  16.7 2.4 %collective-permute-start.2 = (f32[16,128]{1,0:T(8,128)S(1)}, f32[16,128]{1,0:T(8,128)S(1)}, u32[]{:S(2)}, u32[]{:S(2)}) collective-permute-start(f32[16,128]{1,0:T(8,128)S(1)} %get-tuple-element.18), channel_id=1, source_target_pairs={{0,3},{1,0},{2,1},{3,2},{4,7},{5,4},{6,5},{7,6},{8,11},{9,8},{10,9... | collective-permute-start | bytes 24584 | tf_op jit(solution)/shard_map/ppermute | solution.py:208
  19.1 0.0 copy-done.5
  19.1 0.1 pad_maximum_fusion.1.scal
  19.2 0.0 collective-permute-done.1
  19.2 1.2 %collective-permute-done = f32[16,128]{1,0:T(8,128)S(1)} collective-permute-done((f32[16,128]{1,0:T(8,128)S(1)}, f32[16,128]{1,0:T(8,128)S(1)}, u32[]{:S(2)}, u32[]{:S(2)}) %collective-permute-start) | collective-permute-done | bytes 8224 | tf_op jit(solution)/shard_map/ppermute | solution.py:208
  20.4 0.0 collective-permute-done.2
  20.4 2.7 %collective-permute-start.5 = (f32[4,16,128]{2,1,0:T(8,128)S(1)}, f32[4,16,128]{2,1,0:T(8,128)S(1)}, u32[]{:S(2)}, u32[]{:S(2)}) collective-permute-start(f32[4,16,128]{2,1,0:T(8,128)S(1)} %pad_maximum_fusion), channel_id=1, source_target_pairs={{0,12},{1,13},{2,14},{3,15},{4,0},{5,1},{6,2},{7,3},{8,4},{9,5},{1... | collective-permute-start | bytes 98312 | tf_op jit(solution)/shard_map/ppermute | solution.py:211
  23.1 0.3 collective-permute-start.4
  23.5 0.7 collective-permute-start.3
  24.2 3.9 %collective-permute-done.3 = f32[4,16,128]{2,1,0:T(8,128)S(1)} collective-permute-done((f32[4,16,128]{2,1,0:T(8,128)S(1)}, f32[4,16,128]{2,1,0:T(8,128)S(1)}, u32[]{:S(2)}, u32[]{:S(2)}) %collective-permute-start.3) | collective-permute-done | bytes 32800 | tf_op jit(solution)/shard_map/ppermute | solution.py:211
  28.0 0.0 collective-permute-done.4
  28.0 0.0 collective-permute-done.5
  28.1 0.0 copy-done.1
  28.1 2.7 %prep.1 = (bf16[8,576,128]{2,1,0:T(8,128)(2,1)S(1)}, bf16[1152,256]{1,0:T(8,128)(2,1)S(1)}) custom-call(s32[16]{0:T(128)S(1)} %fusion.1.order, f32[16,16,128]{2,1,0:T(8,128)S(1)} %constant_dynamic-update-slice_fusion.tables, f32[9,64,64]{2,1,0:T(8,128)S(1)} %copy-done.1), custom_call_target="tpu_custom_call" | custom-call | bytes 8388608 | tf_op jit(solution)/shard_map/prep/pallas_call | solution.py:216
  30.8 5.0 %all-to-all-done.lines = f32[16,96,128]{2,1,0:T(8,128)S(1)} async-done(((f32[16,96,128]{2,1,0:T(8,128)}), f32[16,96,128]{2,1,0:T(8,128)S(1)}, u32[]{:S(2)}, u32[]{:S(2)}) %all-to-all-start) | async-done | bytes 786464 | tf_op jit(solution)/shard_map/all_to_all | solution.py:198
  35.8 0.0 copy-done
  35.8 1.1 %lines.1 = f32[256,1,384]{2,1,0:T(1,128)S(1)} custom-call(f32[16,96,128]{2,1,0:T(8,128)S(1)} %all-to-all-done.lines, bf16[4,256,256]{2,1,0:T(8,128)(2,1)S(1)} %copy-done), custom_call_target="tpu_custom_call" | custom-call | tf_op jit(solution)/shard_map/lines/pallas_call | solution.py:229
  36.9 27.1 %all_to_all.15 = f32[256,1,384]{2,1,0:T(1,128)S(1)} all-to-all(f32[256,1,384]{2,1,0:T(1,128)S(1)} %lines.1), channel_id=1, replica_groups=mesh['mode'=16,'dom'=16] {'mode','dom'}, dimensions={0} | all-to-all | bytes 786432 | tf_op jit(solution)/shard_map/all_to_all | solution.py:245
  64.0 0.1 copy.14
  64.1 10.5 %solve.1 = f32[16,3,16,128]{3,2,1,0:T(8,128)S(1)} custom-call(f32[9]{0:T(128)S(1)} %pad_maximum_fusion.1.scal, f32[256,384]{1,0:T(8,128)S(1)} %bitcast.26, bf16[8,576,128]{2,1,0:T(8,128)(2,1)S(1)} %get-tuple-element.15.onehot, bf16[1152,256]{1,0:T(8,128)(2,1)S(1)} %get-tuple-element.16.weights), custom_call_target="tpu_custom_call" | custom-call | tf_op jit(solution)/shard_map/solve/pallas_call | solution.py:252
  74.7 12.1 %all_to_all.16 = f32[16,48,128]{2,1,0:T(8,128)S(1)} all-to-all(f32[16,48,128]{2,1,0:T(8,128)S(1)} %bitcast.27), channel_id=1, replica_groups=mesh['mode'=16,'dom'=16] {'dom'}, dimensions={0} | all-to-all | bytes 786432 | tf_op jit(solution)/shard_map/all_to_all | solution.py:260
  86.8 1.0 %reshape.41 = f32[3,8,2,2048]{3,2,1,0:T(2,128)} reshape(f32[3,8,2,16,128]{4,3,2,1,0:T(8,128)S(1)} %bitcast.30) | data formatting | bytes 786432 | tf_op jit(solution)/shard_map/reshape | solution.py:262
  (14 shorter events, 0.1 us)
Async XLA Ops:
  0.0 1.5 %copy-start.2 = (f32[3,8,2,2048]{3,2,1,0:T(2,128)S(1)}, f32[3,8,2,2048]{3,2,1,0:T(2,128)}, u32[]{:S(2)}) copy-start(f32[3,8,2,2048]{3,2,1,0:T(2,128)} %param.8) | copy-start | bytes 1179652
  2.0 11.1 %copy-start.4 = (s32[2,8]{1,0:T(2,128)S(1)}, s32[2,8]{1,0:T(2,128)}, u32[]{:S(2)}) copy-start(s32[2,8]{1,0:T(2,128)} %param.11) | copy-start | bytes 196
  3.0 10.4 %copy-start.3 = (s32[9,32]{1,0:T(8,128)S(1)}, s32[9,32]{1,0:T(8,128)}, u32[]{:S(2)}) copy-start(s32[9,32]{1,0:T(8,128)} %param.10) | copy-start | bytes 3460
  3.0 16.1 %copy-start.5 = (f32[8]{0:T(128)S(1)}, f32[8]{0:T(128)}, u32[]{:S(2)}) copy-start(f32[8]{0:T(128)} %constant.92.clone) | copy-start | bytes 100
  3.0 25.1 %copy-start.1 = (f32[9,64,64]{2,1,0:T(8,128)S(1)}, f32[9,64,64]{2,1,0:T(8,128)}, u32[]{:S(2)}) copy-start(f32[9,64,64]{2,1,0:T(8,128)} %blocks.1) | copy-start | bytes 442372
  3.0 32.8 %copy-start = (bf16[4,256,256]{2,1,0:T(8,128)(2,1)S(1)}, bf16[4,256,256]{2,1,0:T(8,128)(2,1)}, u32[]{:S(2)}) copy-start(bf16[4,256,256]{2,1,0:T(8,128)(2,1)} %constant.91.clone.tables) | copy-start | bytes 1572868
  3.0 32.8 %all-to-all-start = ((f32[16,96,128]{2,1,0:T(8,128)}), f32[16,96,128]{2,1,0:T(8,128)S(1)}, u32[]{:S(2)}, u32[]{:S(2)}) async-start(f32[16,96,128]{2,1,0:T(8,128)} %maximum_bitcast_fusion), calls=%async_computation | async-start | bytes 1572864 | tf_op jit(solution)/shard_map/all_to_all | solution.py:198
  13.5 5.7 %collective-permute-start.1 = (f32[16,128]{1,0:T(8,128)S(1)}, f32[16,128]{1,0:T(8,128)S(1)}, u32[]{:S(2)}, u32[]{:S(2)}) collective-permute-start(f32[16,128]{1,0:T(8,128)S(1)} %get-tuple-element.18), channel_id=1, source_target_pairs={{0,2},{1,3},{2,0},{3,1},{4,6},{5,7},{6,4},{7,5},{8,10},{9,11},{10,... | collective-permute-start | bytes 24584 | tf_op jit(solution)/shard_map/ppermute | solution.py:208
  16.4 4.0 %collective-permute-start = (f32[16,128]{1,0:T(8,128)S(1)}, f32[16,128]{1,0:T(8,128)S(1)}, u32[]{:S(2)}, u32[]{:S(2)}) collective-permute-start(f32[16,128]{1,0:T(8,128)S(1)} %get-tuple-element.18), channel_id=1, source_target_pairs={{0,1},{1,2},{2,3},{3,0},{4,5},{5,6},{6,7},{7,4},{8,9},{9,10},{10,1... | collective-permute-start | bytes 24584 | tf_op jit(solution)/shard_map/ppermute | solution.py:208
  16.7 3.7 %collective-permute-start.2 = (f32[16,128]{1,0:T(8,128)S(1)}, f32[16,128]{1,0:T(8,128)S(1)}, u32[]{:S(2)}, u32[]{:S(2)}) collective-permute-start(f32[16,128]{1,0:T(8,128)S(1)} %get-tuple-element.18), channel_id=1, source_target_pairs={{0,3},{1,0},{2,1},{3,2},{4,7},{5,4},{6,5},{7,6},{8,11},{9,8},{10,9... | collective-permute-start | bytes 24584 | tf_op jit(solution)/shard_map/ppermute | solution.py:208
  20.4 7.7 %collective-permute-start.5 = (f32[4,16,128]{2,1,0:T(8,128)S(1)}, f32[4,16,128]{2,1,0:T(8,128)S(1)}, u32[]{:S(2)}, u32[]{:S(2)}) collective-permute-start(f32[4,16,128]{2,1,0:T(8,128)S(1)} %pad_maximum_fusion), channel_id=1, source_target_pairs={{0,12},{1,13},{2,14},{3,15},{4,0},{5,1},{6,2},{7,3},{8,4},{9,5},{1... | collective-permute-start | bytes 98312 | tf_op jit(solution)/shard_map/ppermute | solution.py:211
  23.1 4.9 %collective-permute-start.4 = (f32[4,16,128]{2,1,0:T(8,128)S(1)}, f32[4,16,128]{2,1,0:T(8,128)S(1)}, u32[]{:S(2)}, u32[]{:S(2)}) collective-permute-start(f32[4,16,128]{2,1,0:T(8,128)S(1)} %pad_maximum_fusion), channel_id=1, source_target_pairs={{0,8},{1,9},{2,10},{3,11},{4,12},{5,13},{6,14},{7,15},{8,0},{9,1},... | collective-permute-start | bytes 98312 | tf_op jit(solution)/shard_map/ppermute | solution.py:211
  23.5 4.6 %collective-permute-start.3 = (f32[4,16,128]{2,1,0:T(8,128)S(1)}, f32[4,16,128]{2,1,0:T(8,128)S(1)}, u32[]{:S(2)}, u32[]{:S(2)}) collective-permute-start(f32[4,16,128]{2,1,0:T(8,128)S(1)} %pad_maximum_fusion), channel_id=1, source_target_pairs={{0,4},{1,5},{2,6},{3,7},{4,8},{5,9},{6,10},{7,11},{8,12},{9,13},{1... | collective-permute-start | bytes 98312 | tf_op jit(solution)/shard_map/ppermute | solution.py:211

commit v4 on v3

--- a/solution.py
+++ b/solution.py
@@ -10,7 +10,7 @@
 
 
 CHEB = 4
-UNROLL = 4
+UNROLL = 8
 NP = 64
 COMPS = 3
 LANES = 128
@@ -44,11 +44,20 @@
     return dot(a[0], b[0]) + dot(a[1], b[0]) + dot(a[0], b[1])
 
 
+def pack_kernel(velocity, vorticity, out):
+    rows = 2 * velocity.shape[0]
+    for i, field in enumerate((velocity, vorticity)):
+        for g in range(0, rows, 8):
+            value = field[g // 2:g // 2 + 4].reshape(8, field.shape[2])
+            for j in range(out.shape[0]):
+                out[j, i * rows + g:i * rows + g + 8, :] = value[:, j * LANES:(j + 1) * LANES]
+
+
 def lines_kernel(lines, tables, out):
     senders, rows, _ = lines.shape
     per = rows // (2 * COMPS)
     count = senders * per
-    fields = [lines[:, i * per:(i + 1) * per, :].reshape(count, LANES) for i in range(2 * COMPS)]
+    fields = [lines[:, (2 * c + i) * per:(2 * c + i + 1) * per, :].reshape(count, LANES) for i in range(2) for c in range(COMPS)]
     forward = (tables[0], tables[1])
     planes = [dot3(forward, split(jnp.concatenate(fields[i:i + 2], axis=1))) for i in range(0, 2 * COMPS, 2)]
     planes = [half for pair in planes for half in (pair[:, :LANES], pair[:, LANES:])]
@@ -146,12 +155,13 @@
             near = ext[pl.ds(pl.multiple_of(g * 2 * elems, 2 * elems), 4 * elems)]
             window = jnp.concatenate([near[:, :2 * LANES], near[:, 2 * LANES:]], axis=0)
             one = onehot[g]
-            y = dot(jnp.concatenate([one, one], axis=1), window)
             for k in range(2):
+                this = one[k * slots * elems:(k + 1) * slots * elems]
+                y = dot(jnp.concatenate([this, this], axis=1), window)
                 two = pl.ds(pl.multiple_of((2 * g + k) * elems, elems), elems)
                 single = pl.ds(pl.multiple_of(twos + (2 * g + k) * pairs, pairs), pairs)
                 for s in range(slots):
-                    row = (k * slots + s) * elems
+                    row = s * elems
                     both = y[row:row + elems, :LANES]
                     last = y[row:row + elems, LANES:]
                     last = jnp.where(few, last[:pairs], last[pairs:])
@@ -194,8 +204,14 @@
     me = lax.axis_index("mode")
     rows = comps * modes_dev * 2
 
-    both = jnp.concatenate([v.reshape(rows, n_mode, LANES) for v in (velocity, vorticity)], axis=0)
-    lines = lax.all_to_all(both.transpose(1, 0, 2), "mode", split_axis=0, concat_axis=0, tiled=True)
+    field = pl.BlockSpec((modes_dev, 2, merged), lambda c: (c, 0, 0))
+    packed = pl.pallas_call(
+        pack_kernel, grid=(comps,),
+        out_shape=jax.ShapeDtypeStruct((n_mode, 2 * rows, LANES), f32),
+        in_specs=[field, field], out_specs=pl.BlockSpec((n_mode, 4 * modes_dev, LANES), lambda c: (0, c, 0)),
+        compiler_params=pltpu.CompilerParams(vmem_limit_bytes=62 << 20), name="pack",
+    )(velocity.reshape(comps * modes_dev, 2, merged), vorticity.reshape(comps * modes_dev, 2, merged))
+    lines = lax.all_to_all(packed, "mode", split_axis=0, concat_axis=0, tiled=True)
 
     table = jnp.concatenate([
         nbr_ref.reshape(slots, pairs, 2).transpose(1, 2, 0).reshape(pairs, 2 * slots),

time: 88 us -> 85.8 us (0.975)
  local copies, waits for them, and re-layouts: 3.53 us -> 1.6 us
  other arithmetic: 1.09 us -> 0.1 us
    pallas_call x0 -> x1, Pallas kernels: none -> 3.01 us  [shards(): pl.pallas_call(pack_kernel, grid=(comps,), out_shape=jax.ShapeDtypeStruct...]
    pallas_call x1, Pallas kernels: 10.5 us -> 8.31 us  [shards(): pl.pallas_call(functools.partial(solve_kernel, parts, pairs, slots), out_...]
    reshape x4 -> x0, local copies, waits for them, and re-layouts: 1.94 us -> none  [shards(): v.reshape(rows, n_mode, LANES)]
    transpose x1 -> x0, other arithmetic: 0.99 us -> none  [shards(): both.transpose(1, 0, 2)]
where the time goes in v4:
time: 85.8 us; the launch traced here: 85.6 us
  blocking collectives  39.1 us (46%)
  starting transfers between devices  19.4 us (23%)
  Pallas kernels  15.1 us (18%)
  waiting for transfers between devices  10.1 us (12%)
  local copies, waits for them, and re-layouts  1.6 us (2%)
    all_to_all x1, blocking collectives, shards(): lax.all_to_all(rhs, ('mode', 'dom'), split_axis=0, concat_axis=0, tiled=T...  27.1 us
    all_to_all x1, blocking collectives, shards(): lax.all_to_all(done.reshape(parts, comps * pairs, LANES), 'dom', split_ax...  12.1 us
    all_to_all x1, starting transfers between devices, shards(): lax.all_to_all(packed, 'mode', split_axis=0, concat_axis=0, tiled=True)  10.1 us
    pallas_call x1, Pallas kernels, shards(): pl.pallas_call(functools.partial(solve_kernel, parts, pairs, slots), out_...  8.31 us
    ppermute x3, starting transfers between devices, shards(): lax.ppermute(table, 'dom', [(d, d // side * side + (d + i) % side) for d...  5.51 us
    all_to_all x1, waiting for transfers between devices, shards(): lax.all_to_all(packed, 'mode', split_axis=0, concat_axis=0, tiled=True)  5.03 us
    ppermute x3, waiting for transfers between devices, shards(): lax.ppermute(table, 'dom', [(d, (d + i * side) % parts) for d in range(pa...  3.87 us
    ppermute x3, starting transfers between devices, shards(): lax.ppermute(table, 'dom', [(d, (d + i * side) % parts) for d in range(pa...  3.78 us
  transfers between devices with their start and end apart: 7, of which 3 were waited for; matrix products, arithmetic and copies ran while one was open for 1% of the time, Pallas kernels for 3%

profile of v4, /device:TPU:1, one launch (start us, length us, event | category | flops | bytes accessed | tf_op | source)
XLA Modules:
  0.0 85.6 jit_solution(9801317363959014325)
XLA Ops:
  0.0 3.0 %pack.1 = f32[16,96,128]{2,1,0:T(8,128)} custom-call(f32[24,2,2048]{2,1,0:T(2,128)} %bitcast.31, f32[24,2,2048]{2,1,0:T(2,128)} %bitcast.32), custom_call_target="tpu_custom_call" | custom-call | tf_op jit(solution)/shard_map/pack/pallas_call | solution.py:208
  3.0 0.0 copy-start.3
  3.0 0.0 copy-start.2
  3.0 0.0 copy-start.4
  3.0 0.0 copy-start.1
  3.0 0.0 copy-start
  3.0 10.1 %all-to-all-start = ((f32[16,96,128]{2,1,0:T(8,128)}), f32[16,96,128]{2,1,0:T(8,128)S(1)}, u32[]{:S(2)}, u32[]{:S(2)}) async-start(f32[16,96,128]{2,1,0:T(8,128)} %pack.1), calls=%async_computation | async-start | bytes 1572864 | tf_op jit(solution)/shard_map/all_to_all | solution.py:214
  13.2 0.0 copy-done.3
  13.2 0.1 reshape.42
  13.2 0.1 pad.11.clone
  13.3 0.1 pad.10.clone
  13.4 0.0 copy-done.2
  13.4 0.1 copy.11
  13.5 0.1 reshape.36
  13.6 2.8 %collective-permute-start.1 = (f32[16,128]{1,0:T(8,128)S(1)}, f32[16,128]{1,0:T(8,128)S(1)}, u32[]{:S(2)}, u32[]{:S(2)}) collective-permute-start(f32[16,128]{1,0:T(8,128)S(1)} %get-tuple-element.18), channel_id=1, source_target_pairs={{0,2},{1,3},{2,0},{3,1},{4,6},{5,7},{6,4},{7,5},{8,10},{9,11},{10,... | collective-permute-start | bytes 24584 | tf_op jit(solution)/shard_map/ppermute | solution.py:224
  16.4 0.3 collective-permute-start
  16.7 2.4 %collective-permute-start.2 = (f32[16,128]{1,0:T(8,128)S(1)}, f32[16,128]{1,0:T(8,128)S(1)}, u32[]{:S(2)}, u32[]{:S(2)}) collective-permute-start(f32[16,128]{1,0:T(8,128)S(1)} %get-tuple-element.18), channel_id=1, source_target_pairs={{0,3},{1,0},{2,1},{3,2},{4,7},{5,4},{6,5},{7,6},{8,11},{9,8},{10,9... | collective-permute-start | bytes 24584 | tf_op jit(solution)/shard_map/ppermute | solution.py:224
  19.2 0.0 copy-done.4
  19.2 0.1 pad_maximum_fusion.1.scal
  19.3 0.0 collective-permute-done.1
  19.3 1.2 %collective-permute-done = f32[16,128]{1,0:T(8,128)S(1)} collective-permute-done((f32[16,128]{1,0:T(8,128)S(1)}, f32[16,128]{1,0:T(8,128)S(1)}, u32[]{:S(2)}, u32[]{:S(2)}) %collective-permute-start) | collective-permute-done | bytes 8224 | tf_op jit(solution)/shard_map/ppermute | solution.py:224
  20.4 0.0 collective-permute-done.2
  20.4 2.7 %collective-permute-start.5 = (f32[4,16,128]{2,1,0:T(8,128)S(1)}, f32[4,16,128]{2,1,0:T(8,128)S(1)}, u32[]{:S(2)}, u32[]{:S(2)}) collective-permute-start(f32[4,16,128]{2,1,0:T(8,128)S(1)} %pad_maximum_fusion), channel_id=1, source_target_pairs={{0,12},{1,13},{2,14},{3,15},{4,0},{5,1},{6,2},{7,3},{8,4},{9,5},{1... | collective-permute-start | bytes 98312 | tf_op jit(solution)/shard_map/ppermute | solution.py:227
  23.2 0.3 collective-permute-start.4
  23.5 0.7 collective-permute-start.3
  24.2 3.9 %collective-permute-done.3 = f32[4,16,128]{2,1,0:T(8,128)S(1)} collective-permute-done((f32[4,16,128]{2,1,0:T(8,128)S(1)}, f32[4,16,128]{2,1,0:T(8,128)S(1)}, u32[]{:S(2)}, u32[]{:S(2)}) %collective-permute-start.3) | collective-permute-done | bytes 32800 | tf_op jit(solution)/shard_map/ppermute | solution.py:227
  28.1 0.0 collective-permute-done.4
  28.1 0.0 collective-permute-done.5
  28.1 0.0 copy-done.1
  28.1 2.7 %prep.1 = (bf16[8,576,128]{2,1,0:T(8,128)(2,1)S(1)}, bf16[1152,256]{1,0:T(8,128)(2,1)S(1)}) custom-call(s32[16]{0:T(128)S(1)} %fusion.1.order, f32[16,16,128]{2,1,0:T(8,128)S(1)} %constant_dynamic-update-slice_fusion.tables, f32[9,64,64]{2,1,0:T(8,128)S(1)} %copy-done.1), custom_call_target="tpu_custom_call" | custom-call | bytes 8388608 | tf_op jit(solution)/shard_map/prep/pallas_call | solution.py:232
  30.9 5.0 %all-to-all-done.lines = f32[16,96,128]{2,1,0:T(8,128)S(1)} async-done(((f32[16,96,128]{2,1,0:T(8,128)}), f32[16,96,128]{2,1,0:T(8,128)S(1)}, u32[]{:S(2)}, u32[]{:S(2)}) %all-to-all-start) | async-done | bytes 786464 | tf_op jit(solution)/shard_map/all_to_all | solution.py:214
  35.9 0.0 copy-done
  35.9 1.0 %lines.1 = f32[256,1,384]{2,1,0:T(1,128)S(1)} custom-call(f32[16,96,128]{2,1,0:T(8,128)S(1)} %all-to-all-done.lines, bf16[4,256,256]{2,1,0:T(8,128)(2,1)S(1)} %copy-done), custom_call_target="tpu_custom_call" | custom-call | tf_op jit(solution)/shard_map/lines/pallas_call | solution.py:245
  36.9 27.1 %all_to_all.15 = f32[256,1,384]{2,1,0:T(1,128)S(1)} all-to-all(f32[256,1,384]{2,1,0:T(1,128)S(1)} %lines.1), channel_id=1, replica_groups=mesh['mode'=16,'dom'=16] {'mode','dom'}, dimensions={0} | all-to-all | bytes 786432 | tf_op jit(solution)/shard_map/all_to_all | solution.py:261
  64.0 0.1 copy.12
  64.2 8.3 %solve.1 = f32[16,3,16,128]{3,2,1,0:T(8,128)S(1)} custom-call(f32[9]{0:T(128)S(1)} %pad_maximum_fusion.1.scal, f32[256,384]{1,0:T(8,128)S(1)} %bitcast.26, bf16[8,576,128]{2,1,0:T(8,128)(2,1)S(1)} %get-tuple-element.15.onehot, bf16[1152,256]{1,0:T(8,128)(2,1)S(1)} %get-tuple-element.16.weights), custom_call_target="tpu_custom_call" | custom-call | tf_op jit(solution)/shard_map/solve/pallas_call | solution.py:268
  72.5 12.1 %all_to_all.16 = f32[16,48,128]{2,1,0:T(8,128)S(1)} all-to-all(f32[16,48,128]{2,1,0:T(8,128)S(1)} %bitcast.27), channel_id=1, replica_groups=mesh['mode'=16,'dom'=16] {'dom'}, dimensions={0} | all-to-all | bytes 786432 | tf_op jit(solution)/shard_map/all_to_all | solution.py:276
  84.6 1.0 %reshape.41 = f32[3,8,2,2048]{3,2,1,0:T(2,128)} reshape(f32[3,8,2,16,128]{4,3,2,1,0:T(8,128)S(1)} %bitcast.30) | data formatting | bytes 786432 | tf_op jit(solution)/shard_map/reshape | solution.py:278
  (14 shorter events, 0.1 us)
Async XLA Ops:
  3.0 10.2 %copy-start.3 = (s32[2,8]{1,0:T(2,128)S(1)}, s32[2,8]{1,0:T(2,128)}, u32[]{:S(2)}) copy-start(s32[2,8]{1,0:T(2,128)} %param.11) | copy-start | bytes 196
  3.0 10.4 %copy-start.2 = (s32[9,32]{1,0:T(8,128)S(1)}, s32[9,32]{1,0:T(8,128)}, u32[]{:S(2)}) copy-start(s32[9,32]{1,0:T(8,128)} %param.10) | copy-start | bytes 3460
  3.0 16.2 %copy-start.4 = (f32[8]{0:T(128)S(1)}, f32[8]{0:T(128)}, u32[]{:S(2)}) copy-start(f32[8]{0:T(128)} %constant.92.clone) | copy-start | bytes 100
  3.0 25.1 %copy-start.1 = (f32[9,64,64]{2,1,0:T(8,128)S(1)}, f32[9,64,64]{2,1,0:T(8,128)}, u32[]{:S(2)}) copy-start(f32[9,64,64]{2,1,0:T(8,128)} %blocks.1) | copy-start | bytes 442372
  3.0 32.9 %copy-start = (bf16[4,256,256]{2,1,0:T(8,128)(2,1)S(1)}, bf16[4,256,256]{2,1,0:T(8,128)(2,1)}, u32[]{:S(2)}) copy-start(bf16[4,256,256]{2,1,0:T(8,128)(2,1)} %constant.91.clone.tables) | copy-start | bytes 1572868
  3.0 32.8 %all-to-all-start = ((f32[16,96,128]{2,1,0:T(8,128)}), f32[16,96,128]{2,1,0:T(8,128)S(1)}, u32[]{:S(2)}, u32[]{:S(2)}) async-start(f32[16,96,128]{2,1,0:T(8,128)} %pack.1), calls=%async_computation | async-start | bytes 1572864 | tf_op jit(solution)/shard_map/all_to_all | solution.py:214
  13.6 5.7 %collective-permute-start.1 = (f32[16,128]{1,0:T(8,128)S(1)}, f32[16,128]{1,0:T(8,128)S(1)}, u32[]{:S(2)}, u32[]{:S(2)}) collective-permute-start(f32[16,128]{1,0:T(8,128)S(1)} %get-tuple-element.18), channel_id=1, source_target_pairs={{0,2},{1,3},{2,0},{3,1},{4,6},{5,7},{6,4},{7,5},{8,10},{9,11},{10,... | collective-permute-start | bytes 24584 | tf_op jit(solution)/shard_map/ppermute | solution.py:224
  16.4 4.0 %collective-permute-start = (f32[16,128]{1,0:T(8,128)S(1)}, f32[16,128]{1,0:T(8,128)S(1)}, u32[]{:S(2)}, u32[]{:S(2)}) collective-permute-start(f32[16,128]{1,0:T(8,128)S(1)} %get-tuple-element.18), channel_id=1, source_target_pairs={{0,1},{1,2},{2,3},{3,0},{4,5},{5,6},{6,7},{7,4},{8,9},{9,10},{10,1... | collective-permute-start | bytes 24584 | tf_op jit(solution)/shard_map/ppermute | solution.py:224
  16.7 3.7 %collective-permute-start.2 = (f32[16,128]{1,0:T(8,128)S(1)}, f32[16,128]{1,0:T(8,128)S(1)}, u32[]{:S(2)}, u32[]{:S(2)}) collective-permute-start(f32[16,128]{1,0:T(8,128)S(1)} %get-tuple-element.18), channel_id=1, source_target_pairs={{0,3},{1,0},{2,1},{3,2},{4,7},{5,4},{6,5},{7,6},{8,11},{9,8},{10,9... | collective-permute-start | bytes 24584 | tf_op jit(solution)/shard_map/ppermute | solution.py:224
  20.4 7.7 %collective-permute-start.5 = (f32[4,16,128]{2,1,0:T(8,128)S(1)}, f32[4,16,128]{2,1,0:T(8,128)S(1)}, u32[]{:S(2)}, u32[]{:S(2)}) collective-permute-start(f32[4,16,128]{2,1,0:T(8,128)S(1)} %pad_maximum_fusion), channel_id=1, source_target_pairs={{0,12},{1,13},{2,14},{3,15},{4,0},{5,1},{6,2},{7,3},{8,4},{9,5},{1... | collective-permute-start | bytes 98312 | tf_op jit(solution)/shard_map/ppermute | solution.py:227
  23.2 4.9 %collective-permute-start.4 = (f32[4,16,128]{2,1,0:T(8,128)S(1)}, f32[4,16,128]{2,1,0:T(8,128)S(1)}, u32[]{:S(2)}, u32[]{:S(2)}) collective-permute-start(f32[4,16,128]{2,1,0:T(8,128)S(1)} %pad_maximum_fusion), channel_id=1, source_target_pairs={{0,8},{1,9},{2,10},{3,11},{4,12},{5,13},{6,14},{7,15},{8,0},{9,1},... | collective-permute-start | bytes 98312 | tf_op jit(solution)/shard_map/ppermute | solution.py:227
  23.5 4.6 %collective-permute-start.3 = (f32[4,16,128]{2,1,0:T(8,128)S(1)}, f32[4,16,128]{2,1,0:T(8,128)S(1)}, u32[]{:S(2)}, u32[]{:S(2)}) collective-permute-start(f32[4,16,128]{2,1,0:T(8,128)S(1)} %pad_maximum_fusion), channel_id=1, source_target_pairs={{0,4},{1,5},{2,6},{3,7},{4,8},{5,9},{6,10},{7,11},{8,12},{9,13},{1... | collective-permute-start | bytes 98312 | tf_op jit(solution)/shard_map/ppermute | solution.py:227

commit v5 on v4

--- a/solution.py
+++ b/solution.py
@@ -27,12 +27,13 @@
     return high, (value - high.astype(np.float64)).astype(np.float32).astype(bf16)
 
 
-def spanwise_tables(count):
+def spanwise_tables(count, senders):
     planes = 2 * count
     angle = 2 * np.pi / planes * ((np.arange(planes)[:, None] * np.arange(count)[None, :]) % planes)
     weights = np.where(np.arange(count) == 0, 1.0, 2.0)
     forward = np.stack([weights * np.cos(angle), -weights * np.sin(angle)], axis=2).reshape(planes, planes)
     back = np.stack([np.cos(angle).T, -np.sin(angle).T], axis=1).reshape(planes, planes) / planes
+    back = back.reshape(senders, -1, planes).swapaxes(0, 1).reshape(planes, planes)
     return np.stack(np_split(forward) + np_split(back))
 
 
@@ -57,18 +58,20 @@
     senders, rows, _ = lines.shape
     per = rows // (2 * COMPS)
     count = senders * per
-    fields = [lines[:, (2 * c + i) * per:(2 * c + i + 1) * per, :].reshape(count, LANES) for i in range(2) for c in range(COMPS)]
+    fields = [lines[:, i * per:(i + 1) * per, :].reshape(count, LANES) for i in range(2 * COMPS)]
     forward = (tables[0], tables[1])
     planes = [dot3(forward, split(jnp.concatenate(fields[i:i + 2], axis=1))) for i in range(0, 2 * COMPS, 2)]
     planes = [half for pair in planes for half in (pair[:, :LANES], pair[:, LANES:])]
     u, w = planes[:COMPS], planes[COMPS:]
     cross = jnp.concatenate([u[(c + 1) % 3] * w[(c + 2) % 3] - u[(c + 2) % 3] * w[(c + 1) % 3] for c in range(3)], axis=1)
     forcing = dot3((tables[2], tables[3]), split(cross))
-    mode = lax.broadcasted_iota(jnp.int32, (count, LANES), 0) >> 1
+    row = lax.broadcasted_iota(jnp.int32, (count, LANES), 0)
+    mode = (row % senders) * (per // 2) + row // (2 * senders)
     wavenum = mode.astype(f32) * (2.0 / count)
     inv_diag = 1.0 / (1.0 + 4.0 * wavenum * wavenum)
     for c in range(COMPS):
-        out[:, 0, c * LANES:(c + 1) * LANES] = (fields[c] + forcing[:, c * LANES:(c + 1) * LANES]) * inv_diag
+        own = jnp.concatenate([lines[:, c * per + k, :] for k in range(per)], axis=0)
+        out[:, 0, c * LANES:(c + 1) * LANES] = (own + forcing[:, c * LANES:(c + 1) * LANES]) * inv_diag
 
 
 def first_send(slots):
@@ -204,11 +207,9 @@
     me = lax.axis_index("mode")
     rows = comps * modes_dev * 2
 
-    field = pl.BlockSpec((modes_dev, 2, merged), lambda c: (c, 0, 0))
     packed = pl.pallas_call(
-        pack_kernel, grid=(comps,),
-        out_shape=jax.ShapeDtypeStruct((n_mode, 2 * rows, LANES), f32),
-        in_specs=[field, field], out_specs=pl.BlockSpec((n_mode, 4 * modes_dev, LANES), lambda c: (0, c, 0)),
+        pack_kernel, out_shape=jax.ShapeDtypeStruct((n_mode, 2 * rows, LANES), f32),
+        in_specs=vmem(2), out_specs=vmem(1)[0],
         compiler_params=pltpu.CompilerParams(vmem_limit_bytes=62 << 20), name="pack",
     )(velocity.reshape(comps * modes_dev, 2, merged), vorticity.reshape(comps * modes_dev, 2, merged))
     lines = lax.all_to_all(packed, "mode", split_axis=0, concat_axis=0, tiled=True)
@@ -247,7 +248,7 @@
         out_shape=jax.ShapeDtypeStruct((devices, 1, width), f32),
         in_specs=vmem(2), out_specs=vmem(1)[0], name="lines",
         compiler_params=pltpu.CompilerParams(vmem_limit_bytes=12 << 20),
-    )(lines, jnp.asarray(spanwise_tables(modes_all)))
+    )(lines, jnp.asarray(spanwise_tables(modes_all, n_mode)))
     mode = me * modes_dev + lax.axis_index("dom") // 2
     wavenum = mode.astype(f32) / modes_all
     coefs = []
@@ -258,8 +259,8 @@
         rho = rho_next
     scal = jnp.concatenate([(1.0 / (1.0 + 4.0 * wavenum * wavenum)).reshape(1), jnp.asarray(coefs, f32)])
     rhs, scal, onehot, weights = lax.optimization_barrier((rhs, scal, onehot, weights))
-    columns = lax.all_to_all(rhs, ("mode", "dom"), split_axis=0, concat_axis=0, tiled=True)
-    columns = columns.reshape(n_mode, parts, width).transpose(1, 0, 2).reshape(devices, width)
+    columns = lax.all_to_all(rhs, ("dom", "mode"), split_axis=0, concat_axis=0, tiled=True)
+    columns = columns.reshape(devices, width)
 
     rows = parts * pairs * 3
     state = pltpu.VMEM((rows, LANES), f32)

time: 85.8 us -> 85.1 us (level)
  no operation moved by 1% of the time
where the time goes in v5:
time: 85.1 us; the launch traced here: 84.8 us
  blocking collectives  39.2 us (46%)
  starting transfers between devices  19.4 us (23%)
  Pallas kernels  14.4 us (17%)
  waiting for transfers between devices  10.1 us (12%)
  local copies, waits for them, and re-layouts  1.47 us (2%)
    all_to_all x1, blocking collectives, shards(): lax.all_to_all(rhs, ('dom', 'mode'), split_axis=0, concat_axis=0, tiled=T...  27.4 us
    all_to_all x1, blocking collectives, shards(): lax.all_to_all(done.reshape(parts, comps * pairs, LANES), 'dom', split_ax...  11.8 us
    all_to_all x1, starting transfers between devices, shards(): lax.all_to_all(packed, 'mode', split_axis=0, concat_axis=0, tiled=True)  10.1 us
    pallas_call x1, Pallas kernels, shards(): pl.pallas_call(functools.partial(solve_kernel, parts, pairs, slots), out_...  8.32 us
    ppermute x3, starting transfers between devices, shards(): lax.ppermute(table, 'dom', [(d, d // side * side + (d + i) % side) for d...  5.51 us
    all_to_all x1, waiting for transfers between devices, shards(): lax.all_to_all(packed, 'mode', split_axis=0, concat_axis=0, tiled=True)  5.03 us
    ppermute x3, waiting for transfers between devices, shards(): lax.ppermute(table, 'dom', [(d, (d + i * side) % parts) for d in range(pa...  3.87 us
    ppermute x3, starting transfers between devices, shards(): lax.ppermute(table, 'dom', [(d, (d + i * side) % parts) for d in range(pa...  3.78 us
  transfers between devices with their start and end apart: 7, of which 3 were waited for; matrix products, arithmetic and copies ran while one was open for 1% of the time, Pallas kernels for 3%

profile of v5, /device:TPU:1, one launch (start us, length us, event | category | flops | bytes accessed | tf_op | source)
XLA Modules:
  0.0 84.8 jit_solution(6805118385375553634)
XLA Ops:
  0.0 2.2 %pack.1 = f32[16,96,128]{2,1,0:T(8,128)} custom-call(f32[24,2,2048]{2,1,0:T(2,128)} %bitcast.29, f32[24,2,2048]{2,1,0:T(2,128)} %bitcast.30), custom_call_target="tpu_custom_call" | custom-call | tf_op jit(solution)/shard_map/pack/pallas_call | solution.py:210
  2.2 0.0 copy-start.3
  2.2 0.0 copy-start.2
  2.2 0.0 copy-start.4
  2.2 0.0 copy-start.1
  2.2 0.0 copy-start
  2.3 10.1 %all-to-all-start = ((f32[16,96,128]{2,1,0:T(8,128)}), f32[16,96,128]{2,1,0:T(8,128)S(1)}, u32[]{:S(2)}, u32[]{:S(2)}) async-start(f32[16,96,128]{2,1,0:T(8,128)} %pack.1), calls=%async_computation | async-start | bytes 1572864 | tf_op jit(solution)/shard_map/all_to_all | solution.py:215
  12.4 0.0 copy-done.3
  12.4 0.1 reshape.38
  12.5 0.1 pad.11.clone
  12.5 0.1 pad.10.clone
  12.6 0.0 copy-done.2
  12.6 0.1 copy.14
  12.7 0.1 reshape.33
  12.8 2.8 %collective-permute-start.1 = (f32[16,128]{1,0:T(8,128)S(1)}, f32[16,128]{1,0:T(8,128)S(1)}, u32[]{:S(2)}, u32[]{:S(2)}) collective-permute-start(f32[16,128]{1,0:T(8,128)S(1)} %get-tuple-element.18), channel_id=1, source_target_pairs={{0,2},{1,3},{2,0},{3,1},{4,6},{5,7},{6,4},{7,5},{8,10},{9,11},{10,... | collective-permute-start | bytes 24584 | tf_op jit(solution)/shard_map/ppermute | solution.py:225
  15.6 0.3 collective-permute-start
  15.9 2.4 %collective-permute-start.2 = (f32[16,128]{1,0:T(8,128)S(1)}, f32[16,128]{1,0:T(8,128)S(1)}, u32[]{:S(2)}, u32[]{:S(2)}) collective-permute-start(f32[16,128]{1,0:T(8,128)S(1)} %get-tuple-element.18), channel_id=1, source_target_pairs={{0,3},{1,0},{2,1},{3,2},{4,7},{5,4},{6,5},{7,6},{8,11},{9,8},{10,9... | collective-permute-start | bytes 24584 | tf_op jit(solution)/shard_map/ppermute | solution.py:225
  18.4 0.0 copy-done.4
  18.4 0.1 pad_maximum_fusion.1.scal
  18.5 0.0 collective-permute-done.1
  18.5 1.2 %collective-permute-done = f32[16,128]{1,0:T(8,128)S(1)} collective-permute-done((f32[16,128]{1,0:T(8,128)S(1)}, f32[16,128]{1,0:T(8,128)S(1)}, u32[]{:S(2)}, u32[]{:S(2)}) %collective-permute-start) | collective-permute-done | bytes 8224 | tf_op jit(solution)/shard_map/ppermute | solution.py:225
  19.6 0.0 collective-permute-done.2
  19.6 2.7 %collective-permute-start.5 = (f32[4,16,128]{2,1,0:T(8,128)S(1)}, f32[4,16,128]{2,1,0:T(8,128)S(1)}, u32[]{:S(2)}, u32[]{:S(2)}) collective-permute-start(f32[4,16,128]{2,1,0:T(8,128)S(1)} %pad_maximum_fusion), channel_id=1, source_target_pairs={{0,12},{1,13},{2,14},{3,15},{4,0},{5,1},{6,2},{7,3},{8,4},{9,5},{1... | collective-permute-start | bytes 98312 | tf_op jit(solution)/shard_map/ppermute | solution.py:228
  22.4 0.3 collective-permute-start.4
  22.7 0.7 collective-permute-start.3
  23.4 3.9 %collective-permute-done.3 = f32[4,16,128]{2,1,0:T(8,128)S(1)} collective-permute-done((f32[4,16,128]{2,1,0:T(8,128)S(1)}, f32[4,16,128]{2,1,0:T(8,128)S(1)}, u32[]{:S(2)}, u32[]{:S(2)}) %collective-permute-start.3) | collective-permute-done | bytes 32800 | tf_op jit(solution)/shard_map/ppermute | solution.py:228
  27.3 0.0 collective-permute-done.4
  27.3 0.0 collective-permute-done.5
  27.3 0.0 copy-done.1
  27.4 2.7 %prep.1 = (bf16[8,576,128]{2,1,0:T(8,128)(2,1)S(1)}, bf16[1152,256]{1,0:T(8,128)(2,1)S(1)}) custom-call(s32[16]{0:T(128)S(1)} %fusion.1.order, f32[16,16,128]{2,1,0:T(8,128)S(1)} %constant_dynamic-update-slice_fusion.tables, f32[9,64,64]{2,1,0:T(8,128)S(1)} %copy-done.1), custom_call_target="tpu_custom_call" | custom-call | bytes 8388608 | tf_op jit(solution)/shard_map/prep/pallas_call | solution.py:233
  30.1 5.0 %all-to-all-done.lines = f32[16,96,128]{2,1,0:T(8,128)S(1)} async-done(((f32[16,96,128]{2,1,0:T(8,128)}), f32[16,96,128]{2,1,0:T(8,128)S(1)}, u32[]{:S(2)}, u32[]{:S(2)}) %all-to-all-start) | async-done | bytes 786464 | tf_op jit(solution)/shard_map/all_to_all | solution.py:215
  35.1 0.0 copy-done
  35.1 1.2 %lines.1 = f32[256,1,384]{2,1,0:T(1,128)S(1)} custom-call(f32[16,96,128]{2,1,0:T(8,128)S(1)} %all-to-all-done.lines, bf16[4,256,256]{2,1,0:T(8,128)(2,1)S(1)} %copy-done), custom_call_target="tpu_custom_call" | custom-call | tf_op jit(solution)/shard_map/lines/pallas_call | solution.py:246
  36.3 27.4 %all_to_all.15 = f32[256,1,384]{2,1,0:T(1,128)S(1)} all-to-all(f32[256,1,384]{2,1,0:T(1,128)S(1)} %lines.1), channel_id=1, replica_groups=mesh['mode'=16,'dom'=16] {'dom','mode'}, dimensions={0} | all-to-all | bytes 786432 | tf_op jit(solution)/shard_map/all_to_all | solution.py:262
  63.7 8.3 %solve.1 = f32[16,3,16,128]{3,2,1,0:T(8,128)S(1)} custom-call(f32[9]{0:T(128)S(1)} %pad_maximum_fusion.1.scal, f32[256,384]{1,0:T(8,128)S(1)} %bitcast.25, bf16[8,576,128]{2,1,0:T(8,128)(2,1)S(1)} %get-tuple-element.15.onehot, bf16[1152,256]{1,0:T(8,128)(2,1)S(1)} %get-tuple-element.16.weights), custom_call_target="tpu_custom_call" | custom-call | tf_op jit(solution)/shard_map/solve/pallas_call | solution.py:269
  72.0 11.8 %all_to_all.16 = f32[16,48,128]{2,1,0:T(8,128)S(1)} all-to-all(f32[16,48,128]{2,1,0:T(8,128)S(1)} %bitcast.26), channel_id=1, replica_groups=mesh['mode'=16,'dom'=16] {'dom'}, dimensions={0} | all-to-all | bytes 786432 | tf_op jit(solution)/shard_map/all_to_all | solution.py:277
  83.9 1.0 %reshape.37 = f32[3,8,2,2048]{3,2,1,0:T(2,128)} reshape(f32[3,8,2,16,128]{4,3,2,1,0:T(8,128)S(1)} %bitcast.28) | data formatting | bytes 786432 | tf_op jit(solution)/shard_map/reshape | solution.py:279
  (14 shorter events, 0.1 us)
Async XLA Ops:
  2.2 10.1 %copy-start.3 = (s32[2,8]{1,0:T(2,128)S(1)}, s32[2,8]{1,0:T(2,128)}, u32[]{:S(2)}) copy-start(s32[2,8]{1,0:T(2,128)} %param.11) | copy-start | bytes 196
  2.2 10.4 %copy-start.2 = (s32[9,32]{1,0:T(8,128)S(1)}, s32[9,32]{1,0:T(8,128)}, u32[]{:S(2)}) copy-start(s32[9,32]{1,0:T(8,128)} %param.10) | copy-start | bytes 3460
  2.2 16.2 %copy-start.4 = (f32[8]{0:T(128)S(1)}, f32[8]{0:T(128)}, u32[]{:S(2)}) copy-start(f32[8]{0:T(128)} %constant.92.clone) | copy-start | bytes 100
  2.2 25.1 %copy-start.1 = (f32[9,64,64]{2,1,0:T(8,128)S(1)}, f32[9,64,64]{2,1,0:T(8,128)}, u32[]{:S(2)}) copy-start(f32[9,64,64]{2,1,0:T(8,128)} %blocks.1) | copy-start | bytes 442372
  2.2 32.9 %copy-start = (bf16[4,256,256]{2,1,0:T(8,128)(2,1)S(1)}, bf16[4,256,256]{2,1,0:T(8,128)(2,1)}, u32[]{:S(2)}) copy-start(bf16[4,256,256]{2,1,0:T(8,128)(2,1)} %constant.91.clone.tables) | copy-start | bytes 1572868
  2.3 32.8 %all-to-all-start = ((f32[16,96,128]{2,1,0:T(8,128)}), f32[16,96,128]{2,1,0:T(8,128)S(1)}, u32[]{:S(2)}, u32[]{:S(2)}) async-start(f32[16,96,128]{2,1,0:T(8,128)} %pack.1), calls=%async_computation | async-start | bytes 1572864 | tf_op jit(solution)/shard_map/all_to_all | solution.py:215
  12.8 5.7 %collective-permute-start.1 = (f32[16,128]{1,0:T(8,128)S(1)}, f32[16,128]{1,0:T(8,128)S(1)}, u32[]{:S(2)}, u32[]{:S(2)}) collective-permute-start(f32[16,128]{1,0:T(8,128)S(1)} %get-tuple-element.18), channel_id=1, source_target_pairs={{0,2},{1,3},{2,0},{3,1},{4,6},{5,7},{6,4},{7,5},{8,10},{9,11},{10,... | collective-permute-start | bytes 24584 | tf_op jit(solution)/shard_map/ppermute | solution.py:225
  15.6 4.0 %collective-permute-start = (f32[16,128]{1,0:T(8,128)S(1)}, f32[16,128]{1,0:T(8,128)S(1)}, u32[]{:S(2)}, u32[]{:S(2)}) collective-permute-start(f32[16,128]{1,0:T(8,128)S(1)} %get-tuple-element.18), channel_id=1, source_target_pairs={{0,1},{1,2},{2,3},{3,0},{4,5},{5,6},{6,7},{7,4},{8,9},{9,10},{10,1... | collective-permute-start | bytes 24584 | tf_op jit(solution)/shard_map/ppermute | solution.py:225
  15.9 3.7 %collective-permute-start.2 = (f32[16,128]{1,0:T(8,128)S(1)}, f32[16,128]{1,0:T(8,128)S(1)}, u32[]{:S(2)}, u32[]{:S(2)}) collective-permute-start(f32[16,128]{1,0:T(8,128)S(1)} %get-tuple-element.18), channel_id=1, source_target_pairs={{0,3},{1,0},{2,1},{3,2},{4,7},{5,4},{6,5},{7,6},{8,11},{9,8},{10,9... | collective-permute-start | bytes 24584 | tf_op jit(solution)/shard_map/ppermute | solution.py:225
  19.6 7.7 %collective-permute-start.5 = (f32[4,16,128]{2,1,0:T(8,128)S(1)}, f32[4,16,128]{2,1,0:T(8,128)S(1)}, u32[]{:S(2)}, u32[]{:S(2)}) collective-permute-start(f32[4,16,128]{2,1,0:T(8,128)S(1)} %pad_maximum_fusion), channel_id=1, source_target_pairs={{0,12},{1,13},{2,14},{3,15},{4,0},{5,1},{6,2},{7,3},{8,4},{9,5},{1... | collective-permute-start | bytes 98312 | tf_op jit(solution)/shard_map/ppermute | solution.py:228
  22.4 4.9 %collective-permute-start.4 = (f32[4,16,128]{2,1,0:T(8,128)S(1)}, f32[4,16,128]{2,1,0:T(8,128)S(1)}, u32[]{:S(2)}, u32[]{:S(2)}) collective-permute-start(f32[4,16,128]{2,1,0:T(8,128)S(1)} %pad_maximum_fusion), channel_id=1, source_target_pairs={{0,8},{1,9},{2,10},{3,11},{4,12},{5,13},{6,14},{7,15},{8,0},{9,1},... | collective-permute-start | bytes 98312 | tf_op jit(solution)/shard_map/ppermute | solution.py:228
  22.7 4.6 %collective-permute-start.3 = (f32[4,16,128]{2,1,0:T(8,128)S(1)}, f32[4,16,128]{2,1,0:T(8,128)S(1)}, u32[]{:S(2)}, u32[]{:S(2)}) collective-permute-start(f32[4,16,128]{2,1,0:T(8,128)S(1)} %pad_maximum_fusion), channel_id=1, source_target_pairs={{0,4},{1,5},{2,6},{3,7},{4,8},{5,9},{6,10},{7,11},{8,12},{9,13},{1... | collective-permute-start | bytes 98312 | tf_op jit(solution)/shard_map/ppermute | solution.py:228

commit v6 on v5

--- a/solution.py
+++ b/solution.py
@@ -45,13 +45,22 @@
     return dot(a[0], b[0]) + dot(a[1], b[0]) + dot(a[0], b[1])
 
 
-def pack_kernel(velocity, vorticity, out):
-    rows = 2 * velocity.shape[0]
+def pack_kernel(velocity, vorticity, out, held, arrived):
+    modes = velocity.shape[0] // COMPS
+    copies = []
     for i, field in enumerate((velocity, vorticity)):
-        for g in range(0, rows, 8):
-            value = field[g // 2:g // 2 + 4].reshape(8, field.shape[2])
+        for c in range(COMPS):
+            at = pl.ds(c * modes, modes)
+            copies.append(pltpu.make_async_copy(field.at[at], held.at[i, at], arrived.at[i * COMPS + c]))
+            copies[-1].start()
+    for i, copy in enumerate(copies):
+        copy.wait()
+        for g in range(0, modes, 4):
+            first = (i % COMPS) * modes + g
+            value = held[i // COMPS, first:first + 4].reshape(8, held.shape[3])
             for j in range(out.shape[0]):
-                out[j, i * rows + g:i * rows + g + 8, :] = value[:, j * LANES:(j + 1) * LANES]
+                at = 2 * (i * modes + g)
+                out[j, at:at + 8, :] = value[:, j * LANES:(j + 1) * LANES]
 
 
 def lines_kernel(lines, tables, out):
@@ -209,10 +218,12 @@
 
     packed = pl.pallas_call(
         pack_kernel, out_shape=jax.ShapeDtypeStruct((n_mode, 2 * rows, LANES), f32),
-        in_specs=vmem(2), out_specs=vmem(1)[0],
+        in_specs=[pl.BlockSpec(memory_space=pl.ANY)] * 2, out_specs=vmem(1)[0],
+        scratch_shapes=[pltpu.VMEM((2, comps * modes_dev, 2, merged), f32), pltpu.SemaphoreType.DMA((2 * comps,))],
         compiler_params=pltpu.CompilerParams(vmem_limit_bytes=62 << 20), name="pack",
     )(velocity.reshape(comps * modes_dev, 2, merged), vorticity.reshape(comps * modes_dev, 2, merged))
-    lines = lax.all_to_all(packed, "mode", split_axis=0, concat_axis=0, tiled=True)
+    lines = lax.all_to_all(packed.reshape(n_mode, 1, 2 * rows * LANES), "mode", split_axis=0, concat_axis=0, tiled=True)
+    lines = lines.reshape(packed.shape)
 
     table = jnp.concatenate([
         nbr_ref.reshape(slots, pairs, 2).transpose(1, 2, 0).reshape(pairs, 2 * slots),
@@ -271,10 +282,11 @@
         out_shape=jax.ShapeDtypeStruct((parts, comps, pairs, LANES), f32),
         in_specs=[pl.BlockSpec(memory_space=pltpu.SMEM)] + vmem(3), out_specs=vmem(1)[0],
         scratch_shapes=[ext, picked, state, state, state],
-        compiler_params=pltpu.CompilerParams(vmem_limit_bytes=24 << 20),
+        compiler_params=pltpu.CompilerParams(
+            vmem_limit_bytes=24 << 20),
         name="solve",
     )(scal, columns, onehot, weights)
-    back = lax.all_to_all(done.reshape(parts, comps * pairs, LANES), "dom", split_axis=0, concat_axis=0, tiled=True)
+    back = lax.all_to_all(done.reshape(parts, 1, comps * pairs * LANES), "dom", split_axis=0, concat_axis=0, tiled=True)
     back = back.reshape(modes_dev, 2, comps, pairs, LANES).transpose(2, 0, 1, 3, 4)
     return back.reshape(comps, modes_dev, 2, merged)
 

time: 85.1 us -> 85.1 us (level)
  no operation moved by 1% of the time
where the time goes in v6:
time: 85.1 us; the launch traced here: 84.8 us
  blocking collectives  39.2 us (46%)
  starting transfers between devices  19.4 us (23%)
  Pallas kernels  14.4 us (17%)
  waiting for transfers between devices  10.1 us (12%)
  local copies, waits for them, and re-layouts  1.48 us (2%)
    all_to_all x1, blocking collectives, shards(): lax.all_to_all(rhs, ('dom', 'mode'), split_axis=0, concat_axis=0, tiled=T...  27.4 us
    all_to_all x1, blocking collectives, shards(): lax.all_to_all(done.reshape(parts, 1, comps * pairs * LANES), 'dom', spli...  11.9 us
    all_to_all x1, starting transfers between devices, shards(): lax.all_to_all(packed.reshape(n_mode, 1, 2 * rows * LANES), 'mode', split...  10.1 us
    pallas_call x1, Pallas kernels, shards(): pl.pallas_call(functools.partial(solve_kernel, parts, pairs, slots), out_...  8.32 us
    ppermute x3, starting transfers between devices, shards(): lax.ppermute(table, 'dom', [(d, d // side * side + (d + i) % side) for d...  5.51 us
    all_to_all x1, waiting for transfers between devices, shards(): lax.all_to_all(packed.reshape(n_mode, 1, 2 * rows * LANES), 'mode', split...  5.03 us
    ppermute x3, waiting for transfers between devices, shards(): lax.ppermute(table, 'dom', [(d, (d + i * side) % parts) for d in range(pa...  3.87 us
    ppermute x3, starting transfers between devices, shards(): lax.ppermute(table, 'dom', [(d, (d + i * side) % parts) for d in range(pa...  3.78 us
  transfers between devices with their start and end apart: 7, of which 3 were waited for; matrix products, arithmetic and copies ran while one was open for 1% of the time, Pallas kernels for 3%

profile of v6, /device:TPU:1, one launch (start us, length us, event | category | flops | bytes accessed | tf_op | source)
XLA Modules:
  0.0 84.8 jit_solution(291347315553245774)
XLA Ops:
  0.0 2.2 %pack.1 = f32[16,96,128]{2,1,0:T(8,128)} custom-call(f32[24,2,2048]{2,1,0:T(2,128)} %bitcast.31, f32[24,2,2048]{2,1,0:T(2,128)} %bitcast.32), custom_call_target="tpu_custom_call" | custom-call | tf_op jit(solution)/shard_map/pack/pallas_call | solution.py:219
  2.2 0.0 copy-start.3
  2.2 0.0 copy-start.2
  2.2 0.0 copy-start.4
  2.2 0.0 copy-start.1
  2.3 0.0 copy-start
  2.3 10.1 %all-to-all-start = ((f32[16,1,12288]{2,1,0:T(1,128)}), f32[16,1,12288]{2,1,0:T(1,128)S(1)}, u32[]{:S(2)}, u32[]{:S(2)}) async-start(f32[16,1,12288]{2,1,0:T(1,128)} %bitcast.29), calls=%async_computation | async-start | bytes 1572864 | tf_op jit(solution)/shard_map/all_to_all | solution.py:225
  12.4 0.0 copy-done.3
  12.4 0.1 reshape.46
  12.5 0.1 pad.11.clone
  12.6 0.1 pad.10.clone
  12.6 0.0 copy-done.2
  12.6 0.1 copy.15
  12.7 0.1 reshape.41
  12.8 2.8 %collective-permute-start.1 = (f32[16,128]{1,0:T(8,128)S(1)}, f32[16,128]{1,0:T(8,128)S(1)}, u32[]{:S(2)}, u32[]{:S(2)}) collective-permute-start(f32[16,128]{1,0:T(8,128)S(1)} %get-tuple-element.18), channel_id=1, source_target_pairs={{0,2},{1,3},{2,0},{3,1},{4,6},{5,7},{6,4},{7,5},{8,10},{9,11},{10,... | collective-permute-start | bytes 24584 | tf_op jit(solution)/shard_map/ppermute | solution.py:236
  15.6 0.3 collective-permute-start
  16.0 2.4 %collective-permute-start.2 = (f32[16,128]{1,0:T(8,128)S(1)}, f32[16,128]{1,0:T(8,128)S(1)}, u32[]{:S(2)}, u32[]{:S(2)}) collective-permute-start(f32[16,128]{1,0:T(8,128)S(1)} %get-tuple-element.18), channel_id=1, source_target_pairs={{0,3},{1,0},{2,1},{3,2},{4,7},{5,4},{6,5},{7,6},{8,11},{9,8},{10,9... | collective-permute-start | bytes 24584 | tf_op jit(solution)/shard_map/ppermute | solution.py:236
  18.4 0.0 copy-done.4
  18.4 0.1 pad_maximum_fusion.1.scal
  18.5 0.0 collective-permute-done.1
  18.5 1.2 %collective-permute-done = f32[16,128]{1,0:T(8,128)S(1)} collective-permute-done((f32[16,128]{1,0:T(8,128)S(1)}, f32[16,128]{1,0:T(8,128)S(1)}, u32[]{:S(2)}, u32[]{:S(2)}) %collective-permute-start) | collective-permute-done | bytes 8224 | tf_op jit(solution)/shard_map/ppermute | solution.py:236
  19.7 0.0 collective-permute-done.2
  19.7 2.7 %collective-permute-start.5 = (f32[4,16,128]{2,1,0:T(8,128)S(1)}, f32[4,16,128]{2,1,0:T(8,128)S(1)}, u32[]{:S(2)}, u32[]{:S(2)}) collective-permute-start(f32[4,16,128]{2,1,0:T(8,128)S(1)} %pad_maximum_fusion), channel_id=1, source_target_pairs={{0,12},{1,13},{2,14},{3,15},{4,0},{5,1},{6,2},{7,3},{8,4},{9,5},{1... | collective-permute-start | bytes 98312 | tf_op jit(solution)/shard_map/ppermute | solution.py:239
  22.4 0.3 collective-permute-start.4
  22.7 0.7 collective-permute-start.3
  23.4 3.9 %collective-permute-done.3 = f32[4,16,128]{2,1,0:T(8,128)S(1)} collective-permute-done((f32[4,16,128]{2,1,0:T(8,128)S(1)}, f32[4,16,128]{2,1,0:T(8,128)S(1)}, u32[]{:S(2)}, u32[]{:S(2)}) %collective-permute-start.3) | collective-permute-done | bytes 32800 | tf_op jit(solution)/shard_map/ppermute | solution.py:239
  27.3 0.0 collective-permute-done.4
  27.3 0.0 collective-permute-done.5
  27.4 0.0 copy-done.1
  27.4 2.7 %prep.1 = (bf16[8,576,128]{2,1,0:T(8,128)(2,1)S(1)}, bf16[1152,256]{1,0:T(8,128)(2,1)S(1)}) custom-call(s32[16]{0:T(128)S(1)} %fusion.1.order, f32[16,16,128]{2,1,0:T(8,128)S(1)} %constant_dynamic-update-slice_fusion.tables, f32[9,64,64]{2,1,0:T(8,128)S(1)} %copy-done.1), custom_call_target="tpu_custom_call" | custom-call | bytes 8388608 | tf_op jit(solution)/shard_map/prep/pallas_call | solution.py:244
  30.1 5.0 %all-to-all-done = f32[16,1,12288]{2,1,0:T(1,128)S(1)} async-done(((f32[16,1,12288]{2,1,0:T(1,128)}), f32[16,1,12288]{2,1,0:T(1,128)S(1)}, u32[]{:S(2)}, u32[]{:S(2)}) %all-to-all-start) | async-done | bytes 786464 | tf_op jit(solution)/shard_map/all_to_all | solution.py:225
  35.1 0.0 copy-done
  35.1 1.2 %lines.1 = f32[256,1,384]{2,1,0:T(1,128)S(1)} custom-call(f32[16,96,128]{2,1,0:T(8,128)S(1)} %bitcast.26, bf16[4,256,256]{2,1,0:T(8,128)(2,1)S(1)} %copy-done), custom_call_target="tpu_custom_call" | custom-call | tf_op jit(solution)/shard_map/lines/pallas_call | solution.py:257
  36.3 27.4 %all_to_all.15 = f32[256,1,384]{2,1,0:T(1,128)S(1)} all-to-all(f32[256,1,384]{2,1,0:T(1,128)S(1)} %lines.1), channel_id=1, replica_groups=mesh['mode'=16,'dom'=16] {'dom','mode'}, dimensions={0} | all-to-all | bytes 786432 | tf_op jit(solution)/shard_map/all_to_all | solution.py:273
  63.7 8.3 %solve.1 = f32[16,3,16,128]{3,2,1,0:T(8,128)S(1)} custom-call(f32[9]{0:T(128)S(1)} %pad_maximum_fusion.1.scal, f32[256,384]{1,0:T(8,128)S(1)} %bitcast.27, bf16[8,576,128]{2,1,0:T(8,128)(2,1)S(1)} %get-tuple-element.15.onehot, bf16[1152,256]{1,0:T(8,128)(2,1)S(1)} %get-tuple-element.16.weights), custom_call_target="tpu_custom_call" | custom-call | tf_op jit(solution)/shard_map/solve/pallas_call | solution.py:280
  72.0 11.9 %all_to_all.16 = f32[16,1,6144]{2,1,0:T(1,128)S(1)} all-to-all(f32[16,1,6144]{2,1,0:T(1,128)S(1)} %bitcast.28), channel_id=1, replica_groups=mesh['mode'=16,'dom'=16] {'dom'}, dimensions={0} | all-to-all | bytes 786432 | tf_op jit(solution)/shard_map/all_to_all | solution.py:289
  83.9 1.0 %reshape.45 = f32[3,8,2,2048]{3,2,1,0:T(2,128)} reshape(f32[3,8,2,16,128]{4,3,2,1,0:T(8,128)S(1)} %copy.17) | data formatting | bytes 786432 | tf_op jit(solution)/shard_map/reshape | solution.py:291
  (14 shorter events, 0.1 us)
Async XLA Ops:
  2.2 10.2 %copy-start.3 = (s32[2,8]{1,0:T(2,128)S(1)}, s32[2,8]{1,0:T(2,128)}, u32[]{:S(2)}) copy-start(s32[2,8]{1,0:T(2,128)} %param.11) | copy-start | bytes 196
  2.2 10.4 %copy-start.2 = (s32[9,32]{1,0:T(8,128)S(1)}, s32[9,32]{1,0:T(8,128)}, u32[]{:S(2)}) copy-start(s32[9,32]{1,0:T(8,128)} %param.10) | copy-start | bytes 3460
  2.2 16.2 %copy-start.4 = (f32[8]{0:T(128)S(1)}, f32[8]{0:T(128)}, u32[]{:S(2)}) copy-start(f32[8]{0:T(128)} %constant.92.clone) | copy-start | bytes 100
  2.2 25.1 %copy-start.1 = (f32[9,64,64]{2,1,0:T(8,128)S(1)}, f32[9,64,64]{2,1,0:T(8,128)}, u32[]{:S(2)}) copy-start(f32[9,64,64]{2,1,0:T(8,128)} %blocks.1) | copy-start | bytes 442372
  2.3 32.9 %copy-start = (bf16[4,256,256]{2,1,0:T(8,128)(2,1)S(1)}, bf16[4,256,256]{2,1,0:T(8,128)(2,1)}, u32[]{:S(2)}) copy-start(bf16[4,256,256]{2,1,0:T(8,128)(2,1)} %constant.91.clone.tables) | copy-start | bytes 1572868
  2.3 32.8 %all-to-all-start = ((f32[16,1,12288]{2,1,0:T(1,128)}), f32[16,1,12288]{2,1,0:T(1,128)S(1)}, u32[]{:S(2)}, u32[]{:S(2)}) async-start(f32[16,1,12288]{2,1,0:T(1,128)} %bitcast.29), calls=%async_computation | async-start | bytes 1572864 | tf_op jit(solution)/shard_map/all_to_all | solution.py:225
  12.8 5.7 %collective-permute-start.1 = (f32[16,128]{1,0:T(8,128)S(1)}, f32[16,128]{1,0:T(8,128)S(1)}, u32[]{:S(2)}, u32[]{:S(2)}) collective-permute-start(f32[16,128]{1,0:T(8,128)S(1)} %get-tuple-element.18), channel_id=1, source_target_pairs={{0,2},{1,3},{2,0},{3,1},{4,6},{5,7},{6,4},{7,5},{8,10},{9,11},{10,... | collective-permute-start | bytes 24584 | tf_op jit(solution)/shard_map/ppermute | solution.py:236
  15.6 4.0 %collective-permute-start = (f32[16,128]{1,0:T(8,128)S(1)}, f32[16,128]{1,0:T(8,128)S(1)}, u32[]{:S(2)}, u32[]{:S(2)}) collective-permute-start(f32[16,128]{1,0:T(8,128)S(1)} %get-tuple-element.18), channel_id=1, source_target_pairs={{0,1},{1,2},{2,3},{3,0},{4,5},{5,6},{6,7},{7,4},{8,9},{9,10},{10,1... | collective-permute-start | bytes 24584 | tf_op jit(solution)/shard_map/ppermute | solution.py:236
  16.0 3.7 %collective-permute-start.2 = (f32[16,128]{1,0:T(8,128)S(1)}, f32[16,128]{1,0:T(8,128)S(1)}, u32[]{:S(2)}, u32[]{:S(2)}) collective-permute-start(f32[16,128]{1,0:T(8,128)S(1)} %get-tuple-element.18), channel_id=1, source_target_pairs={{0,3},{1,0},{2,1},{3,2},{4,7},{5,4},{6,5},{7,6},{8,11},{9,8},{10,9... | collective-permute-start | bytes 24584 | tf_op jit(solution)/shard_map/ppermute | solution.py:236
  19.7 7.7 %collective-permute-start.5 = (f32[4,16,128]{2,1,0:T(8,128)S(1)}, f32[4,16,128]{2,1,0:T(8,128)S(1)}, u32[]{:S(2)}, u32[]{:S(2)}) collective-permute-start(f32[4,16,128]{2,1,0:T(8,128)S(1)} %pad_maximum_fusion), channel_id=1, source_target_pairs={{0,12},{1,13},{2,14},{3,15},{4,0},{5,1},{6,2},{7,3},{8,4},{9,5},{1... | collective-permute-start | bytes 98312 | tf_op jit(solution)/shard_map/ppermute | solution.py:239
  22.4 4.9 %collective-permute-start.4 = (f32[4,16,128]{2,1,0:T(8,128)S(1)}, f32[4,16,128]{2,1,0:T(8,128)S(1)}, u32[]{:S(2)}, u32[]{:S(2)}) collective-permute-start(f32[4,16,128]{2,1,0:T(8,128)S(1)} %pad_maximum_fusion), channel_id=1, source_target_pairs={{0,8},{1,9},{2,10},{3,11},{4,12},{5,13},{6,14},{7,15},{8,0},{9,1},... | collective-permute-start | bytes 98312 | tf_op jit(solution)/shard_map/ppermute | solution.py:239
  22.7 4.6 %collective-permute-start.3 = (f32[4,16,128]{2,1,0:T(8,128)S(1)}, f32[4,16,128]{2,1,0:T(8,128)S(1)}, u32[]{:S(2)}, u32[]{:S(2)}) collective-permute-start(f32[4,16,128]{2,1,0:T(8,128)S(1)} %pad_maximum_fusion), channel_id=1, source_target_pairs={{0,4},{1,5},{2,6},{3,7},{4,8},{5,9},{6,10},{7,11},{8,12},{9,13},{1... | collective-permute-start | bytes 98312 | tf_op jit(solution)/shard_map/ppermute | solution.py:239

commit v7 on v6

--- a/solution.py
+++ b/solution.py
@@ -87,10 +87,12 @@
     return -(-2 * slots // 8) * 8
 
 
-def prep_kernel(parts, pairs, slots, send, order, tables, blocks, onehot, weights, refs_at, kap):
+def prep_kernel(parts, pairs, slots, send, order, *refs):
+    *tables, onehot, refs_at, kap = refs
     elems = 2 * pairs
+    side = parts // len(tables)
     for k in range(parts):
-        refs_at[pl.ds(pl.multiple_of(order[k] * pairs, pairs), pairs), :] = tables[k]
+        refs_at[pl.ds(pl.multiple_of(order[k] * pairs, pairs), pairs), :] = tables[k // side][k % side]
 
     turned = refs_at[...].T
     first = first_send(slots)
@@ -120,8 +122,10 @@
                 onehot[d >> 1, pl.ds(at, pairs), :] = hit
         return carry
 
-    lax.fori_loop(0, parts, build, 0, unroll=4)
-
+    lax.fori_loop(0, parts, build, 0, unroll=parts)
+
+
+def weight_kernel(slots, blocks, weights):
     weights[...] = jnp.zeros_like(weights)
 
     def place_block(s, carry):
@@ -132,7 +136,7 @@
                 weights[pl.ds(base + c * NP, NP), at:at + NP] = val
         return carry
 
-    lax.fori_loop(0, slots, place_block, 0, unroll=3)
+    lax.fori_loop(0, slots, place_block, 0, unroll=slots)
 
 
 def solve_kernel(parts, pairs, slots, scal, state_in, onehot, weights, out,
@@ -238,19 +242,26 @@
     table = jnp.stack([table] + near)
     far = [lax.ppermute(table, "dom", [(d, (d + i * side) % parts) for d in range(parts)])
            for i in range(1, parts // side)]
-    table = jnp.concatenate([table] + far, axis=0)
+    tables = [table] + far
     steps = jnp.arange(parts, dtype=jnp.int32)
     order = (here // side - steps // side) % (parts // side) * side + (here % side - steps % side) % side
-    onehot, weights = pl.pallas_call(
+    onehot = pl.pallas_call(
         functools.partial(prep_kernel, parts, pairs, slots, send),
-        out_shape=[jax.ShapeDtypeStruct((parts // 2, 2 * slots * elems, LANES), bf16),
-                   jax.ShapeDtypeStruct((slots * LANES, 2 * LANES), bf16)],
-        in_specs=[pl.BlockSpec(memory_space=pltpu.SMEM)] + vmem(2), out_specs=vmem(2),
+        out_shape=jax.ShapeDtypeStruct((parts // 2, 2 * slots * elems, LANES), bf16),
+        in_specs=[pl.BlockSpec(memory_space=pltpu.SMEM)] + vmem(len(tables)), out_specs=vmem(1)[0],
         scratch_shapes=[pltpu.VMEM((parts * pairs, LANES), f32), pltpu.VMEM((parts * pairs, LANES), jnp.int32)],
         compiler_params=pltpu.CompilerParams(vmem_limit_bytes=8 << 20),
         cost_estimate=pl.CostEstimate(flops=0, bytes_accessed=8 << 20, transcendentals=0),
         name="prep",
-    )(order, table, blocks)
+    )(order, *tables)
+    weights = pl.pallas_call(
+        functools.partial(weight_kernel, slots),
+        out_shape=jax.ShapeDtypeStruct((slots * LANES, 2 * LANES), bf16),
+        in_specs=vmem(1), out_specs=vmem(1)[0],
+        compiler_params=pltpu.CompilerParams(vmem_limit_bytes=4 << 20),
+        cost_estimate=pl.CostEstimate(flops=0, bytes_accessed=1 << 20, transcendentals=0),
+        name="weights",
+    )(blocks)
 
     width = comps * LANES
     devices = n_mode * parts

time: 85.1 us -> 84.9 us (level)
    all_to_all x1, waiting for transfers between devices: 5.03 us -> 5.94 us  [shards(): lax.all_to_all(packed.reshape(n_mode, 1, 2 * rows * LANES), 'mode', split...]
    pallas_call x1, Pallas kernels: 2.71 us -> 1.83 us  [shards(): pl.pallas_call(functools.partial(prep_kernel, parts, pairs, slots, send),...]
  transfers between devices with their start and end apart: 7 -> 7, of which waited for: 3 -> 4; matrix products, arithmetic and copies ran while one was open for 1% -> 1% of each run, Pallas kernels for 3% -> 3%
where the time goes in v7:
time: 84.9 us; the launch traced here: 84.7 us
  blocking collectives  39.1 us (46%)
  starting transfers between devices  19.4 us (23%)
  Pallas kernels  13.8 us (16%)
  waiting for transfers between devices  10.7 us (13%)
  local copies, waits for them, and re-layouts  1.45 us (2%)
    all_to_all x1, blocking collectives, shards(): lax.all_to_all(rhs, ('dom', 'mode'), split_axis=0, concat_axis=0, tiled=T...  27.3 us
    all_to_all x1, blocking collectives, shards(): lax.all_to_all(done.reshape(parts, 1, comps * pairs * LANES), 'dom', spli...  11.9 us
    all_to_all x1, starting transfers between devices, shards(): lax.all_to_all(packed.reshape(n_mode, 1, 2 * rows * LANES), 'mode', split...  10.1 us
    pallas_call x1, Pallas kernels, shards(): pl.pallas_call(functools.partial(solve_kernel, parts, pairs, slots), out_...  8.28 us
    all_to_all x1, waiting for transfers between devices, shards(): lax.all_to_all(packed.reshape(n_mode, 1, 2 * rows * LANES), 'mode', split...  5.94 us
    ppermute x3, starting transfers between devices, shards(): lax.ppermute(table, 'dom', [(d, d // side * side + (d + i) % side) for d...  5.51 us
    ppermute x3, starting transfers between devices, shards(): lax.ppermute(table, 'dom', [(d, (d + i * side) % parts) for d in range(pa...  3.78 us
    ppermute x3, waiting for transfers between devices, shards(): lax.ppermute(table, 'dom', [(d, (d + i * side) % parts) for d in range(pa...  3.47 us
  transfers between devices with their start and end apart: 7, of which 4 were waited for; matrix products, arithmetic and copies ran while one was open for 1% of the time, Pallas kernels for 3%

profile of v7, /device:TPU:1, one launch (start us, length us, event | category | flops | bytes accessed | tf_op | source)
XLA Modules:
  0.0 84.7 jit_solution(15860957933582370370)
XLA Ops:
  0.0 2.2 %pack.1 = f32[16,96,128]{2,1,0:T(8,128)} custom-call(f32[24,2,2048]{2,1,0:T(2,128)} %bitcast.27, f32[24,2,2048]{2,1,0:T(2,128)} %bitcast.28), custom_call_target="tpu_custom_call" | custom-call | tf_op jit(solution)/shard_map/pack/pallas_call | solution.py:223
  2.2 0.0 copy-start.3
  2.2 0.0 copy-start.2
  2.2 0.0 copy-start.4
  2.2 0.0 copy-start.1
  2.2 10.1 %all-to-all-start = ((f32[16,1,12288]{2,1,0:T(1,128)}), f32[16,1,12288]{2,1,0:T(1,128)S(1)}, u32[]{:S(2)}, u32[]{:S(2)}) async-start(f32[16,1,12288]{2,1,0:T(1,128)} %bitcast.25), calls=%async_computation | async-start | bytes 1572864 | tf_op jit(solution)/shard_map/all_to_all | solution.py:229
  12.4 0.0 copy-done.3
  12.4 0.1 reshape.46
  12.4 0.1 pad.11.clone
  12.5 0.1 pad.10.clone
  12.6 0.0 copy-done.2
  12.6 0.1 copy.15
  12.7 0.1 reshape.41
  12.8 0.0 copy-start
  12.8 2.8 %collective-permute-start.1 = (f32[16,128]{1,0:T(8,128)S(1)}, f32[16,128]{1,0:T(8,128)S(1)}, u32[]{:S(2)}, u32[]{:S(2)}) collective-permute-start(f32[16,128]{1,0:T(8,128)S(1)} %get-tuple-element.14), channel_id=1, source_target_pairs={{0,2},{1,3},{2,0},{3,1},{4,6},{5,7},{6,4},{7,5},{8,10},{9,11},{10,... | collective-permute-start | bytes 24584 | tf_op jit(solution)/shard_map/ppermute | solution.py:240
  15.6 0.3 collective-permute-start
  15.9 2.4 %collective-permute-start.2 = (f32[16,128]{1,0:T(8,128)S(1)}, f32[16,128]{1,0:T(8,128)S(1)}, u32[]{:S(2)}, u32[]{:S(2)}) collective-permute-start(f32[16,128]{1,0:T(8,128)S(1)} %get-tuple-element.14), channel_id=1, source_target_pairs={{0,3},{1,0},{2,1},{3,2},{4,7},{5,4},{6,5},{7,6},{8,11},{9,8},{10,9... | collective-permute-start | bytes 24584 | tf_op jit(solution)/shard_map/ppermute | solution.py:240
  18.4 0.0 collective-permute-done.1
  18.4 1.2 %collective-permute-done = f32[16,128]{1,0:T(8,128)S(1)} collective-permute-done((f32[16,128]{1,0:T(8,128)S(1)}, f32[16,128]{1,0:T(8,128)S(1)}, u32[]{:S(2)}, u32[]{:S(2)}) %collective-permute-start) | collective-permute-done | bytes 8224 | tf_op jit(solution)/shard_map/ppermute | solution.py:240
  19.6 0.0 collective-permute-done.2
  19.6 2.7 %collective-permute-start.5 = (f32[4,16,128]{2,1,0:T(8,128)S(1)}, f32[4,16,128]{2,1,0:T(8,128)S(1)}, u32[]{:S(2)}, u32[]{:S(2)}) collective-permute-start(f32[4,16,128]{2,1,0:T(8,128)S(1)} %pad_maximum_fusion.refs_0_), channel_id=1, source_target_pairs={{0,12},{1,13},{2,14},{3,15},{4,0},{5,1},{6,2},{7,3},{8,4},{9,5},{1... | collective-permute-start | bytes 98312 | tf_op jit(solution)/shard_map/ppermute | solution.py:243
  22.4 0.3 collective-permute-start.4
  22.7 0.7 collective-permute-start.3
  23.4 0.0 copy-done.4
  23.4 0.1 pad_maximum_fusion.1.scal
  23.5 0.0 copy-done.1
  23.5 0.3 weights.1
  23.8 0.0 collective-permute-done.5.refs_3_
  23.8 3.1 %collective-permute-done.4.refs_2_ = f32[4,16,128]{2,1,0:T(8,128)S(1)} collective-permute-done((f32[4,16,128]{2,1,0:T(8,128)S(1)}, f32[4,16,128]{2,1,0:T(8,128)S(1)}, u32[]{:S(2)}, u32[]{:S(2)}) %collective-permute-start.4) | collective-permute-done | bytes 32800 | tf_op jit(solution)/shard_map/ppermute | solution.py:243
  26.9 0.4 collective-permute-done.3.refs_1_
  27.3 1.8 %prep.1.onehot = bf16[8,576,128]{2,1,0:T(8,128)(2,1)S(1)} custom-call(s32[16]{0:T(128)S(1)} %fusion.1.order, f32[4,16,128]{2,1,0:T(8,128)S(1)} %pad_maximum_fusion.refs_0_, f32[4,16,128]{2,1,0:T(8,128)S(1)} %collective-permute-done.3.refs_1_, f32[4,16,128]{2,1,0:T(8,128)S(1)} %collective-permute-done.4.refs_2_, f32[4,16,128]{2,1,0:T(8,128)S(1)} %collective-permute-done.5.refs_3_), custom_call_target="tpu_custom_call" | custom-call | bytes 8388608 | tf_op jit(solution)/shard_map/prep/pallas_call | solution.py:248
  29.1 5.9 %all-to-all-done = f32[16,1,12288]{2,1,0:T(1,128)S(1)} async-done(((f32[16,1,12288]{2,1,0:T(1,128)}), f32[16,1,12288]{2,1,0:T(1,128)S(1)}, u32[]{:S(2)}, u32[]{:S(2)}) %all-to-all-start) | async-done | bytes 786464 | tf_op jit(solution)/shard_map/all_to_all | solution.py:229
  35.1 0.0 copy-done
  35.1 1.2 %lines.1 = f32[256,1,384]{2,1,0:T(1,128)S(1)} custom-call(f32[16,96,128]{2,1,0:T(8,128)S(1)} %bitcast.22, bf16[4,256,256]{2,1,0:T(8,128)(2,1)S(1)} %copy-done), custom_call_target="tpu_custom_call" | custom-call | tf_op jit(solution)/shard_map/lines/pallas_call | solution.py:268
  36.2 27.3 %all_to_all.15 = f32[256,1,384]{2,1,0:T(1,128)S(1)} all-to-all(f32[256,1,384]{2,1,0:T(1,128)S(1)} %lines.1), channel_id=1, replica_groups=mesh['mode'=16,'dom'=16] {'dom','mode'}, dimensions={0} | all-to-all | bytes 786432 | tf_op jit(solution)/shard_map/all_to_all | solution.py:284
  63.5 8.3 %solve.1 = f32[16,3,16,128]{3,2,1,0:T(8,128)S(1)} custom-call(f32[9]{0:T(128)S(1)} %pad_maximum_fusion.1.scal, f32[256,384]{1,0:T(8,128)S(1)} %bitcast.23, bf16[8,576,128]{2,1,0:T(8,128)(2,1)S(1)} %prep.1.onehot, bf16[1152,256]{1,0:T(8,128)(2,1)S(1)} %weights.1), custom_call_target="tpu_custom_call" | custom-call | tf_op jit(solution)/shard_map/solve/pallas_call | solution.py:291
  71.8 11.9 %all_to_all.16 = f32[16,1,6144]{2,1,0:T(1,128)S(1)} all-to-all(f32[16,1,6144]{2,1,0:T(1,128)S(1)} %bitcast.24), channel_id=1, replica_groups=mesh['mode'=16,'dom'=16] {'dom'}, dimensions={0} | all-to-all | bytes 786432 | tf_op jit(solution)/shard_map/all_to_all | solution.py:300
  83.7 1.0 %reshape.45 = f32[3,8,2,2048]{3,2,1,0:T(2,128)} reshape(f32[3,8,2,16,128]{4,3,2,1,0:T(8,128)S(1)} %copy.17) | data formatting | bytes 786432 | tf_op jit(solution)/shard_map/reshape | solution.py:302
  (7 shorter events, 0.1 us)
Async XLA Ops:
  2.2 10.2 %copy-start.3 = (s32[2,8]{1,0:T(2,128)S(1)}, s32[2,8]{1,0:T(2,128)}, u32[]{:S(2)}) copy-start(s32[2,8]{1,0:T(2,128)} %param.11) | copy-start | bytes 196
  2.2 10.4 %copy-start.2 = (s32[9,32]{1,0:T(8,128)S(1)}, s32[9,32]{1,0:T(8,128)}, u32[]{:S(2)}) copy-start(s32[9,32]{1,0:T(8,128)} %param.10) | copy-start | bytes 3460
  2.2 21.2 %copy-start.4 = (f32[8]{0:T(128)S(1)}, f32[8]{0:T(128)}, u32[]{:S(2)}) copy-start(f32[8]{0:T(128)} %constant.92.clone) | copy-start | bytes 100
  2.2 21.3 %copy-start.1 = (f32[9,64,64]{2,1,0:T(8,128)S(1)}, f32[9,64,64]{2,1,0:T(8,128)}, u32[]{:S(2)}) copy-start(f32[9,64,64]{2,1,0:T(8,128)} %blocks.1) | copy-start | bytes 442372
  2.2 32.8 %all-to-all-start = ((f32[16,1,12288]{2,1,0:T(1,128)}), f32[16,1,12288]{2,1,0:T(1,128)S(1)}, u32[]{:S(2)}, u32[]{:S(2)}) async-start(f32[16,1,12288]{2,1,0:T(1,128)} %bitcast.25), calls=%async_computation | async-start | bytes 1572864 | tf_op jit(solution)/shard_map/all_to_all | solution.py:229
  12.8 22.3 %copy-start = (bf16[4,256,256]{2,1,0:T(8,128)(2,1)S(1)}, bf16[4,256,256]{2,1,0:T(8,128)(2,1)}, u32[]{:S(2)}) copy-start(bf16[4,256,256]{2,1,0:T(8,128)(2,1)} %constant.91.clone.tables) | copy-start | bytes 1572868
  12.8 5.6 %collective-permute-start.1 = (f32[16,128]{1,0:T(8,128)S(1)}, f32[16,128]{1,0:T(8,128)S(1)}, u32[]{:S(2)}, u32[]{:S(2)}) collective-permute-start(f32[16,128]{1,0:T(8,128)S(1)} %get-tuple-element.14), channel_id=1, source_target_pairs={{0,2},{1,3},{2,0},{3,1},{4,6},{5,7},{6,4},{7,5},{8,10},{9,11},{10,... | collective-permute-start | bytes 24584 | tf_op jit(solution)/shard_map/ppermute | solution.py:240
  15.6 4.0 %collective-permute-start = (f32[16,128]{1,0:T(8,128)S(1)}, f32[16,128]{1,0:T(8,128)S(1)}, u32[]{:S(2)}, u32[]{:S(2)}) collective-permute-start(f32[16,128]{1,0:T(8,128)S(1)} %get-tuple-element.14), channel_id=1, source_target_pairs={{0,1},{1,2},{2,3},{3,0},{4,5},{5,6},{6,7},{7,4},{8,9},{9,10},{10,1... | collective-permute-start | bytes 24584 | tf_op jit(solution)/shard_map/ppermute | solution.py:240
  15.9 3.7 %collective-permute-start.2 = (f32[16,128]{1,0:T(8,128)S(1)}, f32[16,128]{1,0:T(8,128)S(1)}, u32[]{:S(2)}, u32[]{:S(2)}) collective-permute-start(f32[16,128]{1,0:T(8,128)S(1)} %get-tuple-element.14), channel_id=1, source_target_pairs={{0,3},{1,0},{2,1},{3,2},{4,7},{5,4},{6,5},{7,6},{8,11},{9,8},{10,9... | collective-permute-start | bytes 24584 | tf_op jit(solution)/shard_map/ppermute | solution.py:240
  19.6 4.2 %collective-permute-start.5 = (f32[4,16,128]{2,1,0:T(8,128)S(1)}, f32[4,16,128]{2,1,0:T(8,128)S(1)}, u32[]{:S(2)}, u32[]{:S(2)}) collective-permute-start(f32[4,16,128]{2,1,0:T(8,128)S(1)} %pad_maximum_fusion.refs_0_), channel_id=1, source_target_pairs={{0,12},{1,13},{2,14},{3,15},{4,0},{5,1},{6,2},{7,3},{8,4},{9,5},{1... | collective-permute-start | bytes 98312 | tf_op jit(solution)/shard_map/ppermute | solution.py:243
  22.4 4.5 %collective-permute-start.4 = (f32[4,16,128]{2,1,0:T(8,128)S(1)}, f32[4,16,128]{2,1,0:T(8,128)S(1)}, u32[]{:S(2)}, u32[]{:S(2)}) collective-permute-start(f32[4,16,128]{2,1,0:T(8,128)S(1)} %pad_maximum_fusion.refs_0_), channel_id=1, source_target_pairs={{0,8},{1,9},{2,10},{3,11},{4,12},{5,13},{6,14},{7,15},{8,0},{9,1},... | collective-permute-start | bytes 98312 | tf_op jit(solution)/shard_map/ppermute | solution.py:243
  22.7 4.6 %collective-permute-start.3 = (f32[4,16,128]{2,1,0:T(8,128)S(1)}, f32[4,16,128]{2,1,0:T(8,128)S(1)}, u32[]{:S(2)}, u32[]{:S(2)}) collective-permute-start(f32[4,16,128]{2,1,0:T(8,128)S(1)} %pad_maximum_fusion.refs_0_), channel_id=1, source_target_pairs={{0,4},{1,5},{2,6},{3,7},{4,8},{5,9},{6,10},{7,11},{8,12},{9,13},{1... | collective-permute-start | bytes 98312 | tf_op jit(solution)/shard_map/ppermute | solution.py:243

commit v8 on v7

--- a/solution.py
+++ b/solution.py
@@ -154,7 +154,7 @@
     dirn[:twos] = halves(jnp.where(half, x[0], pltpu.roll(x[1], NP, 1)), jnp.where(half, pltpu.roll(x[0], NP, 1), x[1]))
     dirn[twos:] = x[2]
     resid[...] = dirn[...]
-    sol[...] = jnp.zeros_like(sol)
+    sol[...] = dirn[...]
     inv_diag = scal[0]
 
     def step(i, carry):
@@ -191,14 +191,15 @@
         total = dot(picked[...], jnp.concatenate([weights[...], weights[...]], axis=0))
         total = total[:, :LANES] + total[:, LANES:]
         old = dirn[...]
-        sol[...] = sol[...] + old
         left = resid[...] - (old + inv_diag * total)
         resid[...] = left
-        dirn[...] = scal[1 + 2 * i] * old + scal[2 + 2 * i] * left
+        new = scal[1 + 2 * i] * old + scal[2 + 2 * i] * left
+        dirn[...] = new
+        sol[...] = sol[...] + new
         return carry
 
     lax.fori_loop(0, CHEB, step, 0)
-    final = sol[...] + dirn[...]
+    final = sol[...]
     both = final[:twos].reshape(parts, 2, pairs, LANES)
     a = [both[:, h].reshape(ones, LANES) for h in range(2)]
     out[:, 0] = jnp.where(half, a[0], pltpu.roll(a[1], NP, 1)).reshape(shape)

time: 84.9 us -> 84.9 us (level)
  no operation moved by 1% of the time
where the time goes in v8:
time: 84.9 us; the launch traced here: 84.7 us
  blocking collectives  39.1 us (46%)
  starting transfers between devices  19.4 us (23%)
  Pallas kernels  13.8 us (16%)
  waiting for transfers between devices  10.7 us (13%)
  local copies, waits for them, and re-layouts  1.45 us (2%)
    all_to_all x1, blocking collectives, shards(): lax.all_to_all(rhs, ('dom', 'mode'), split_axis=0, concat_axis=0, tiled=T...  27.3 us
    all_to_all x1, blocking collectives, shards(): lax.all_to_all(done.reshape(parts, 1, comps * pairs * LANES), 'dom', spli...  11.9 us
    all_to_all x1, starting transfers between devices, shards(): lax.all_to_all(packed.reshape(n_mode, 1, 2 * rows * LANES), 'mode', split...  10.1 us
    pallas_call x1, Pallas kernels, shards(): pl.pallas_call(functools.partial(solve_kernel, parts, pairs, slots), out_...  8.29 us
    all_to_all x1, waiting for transfers between devices, shards(): lax.all_to_all(packed.reshape(n_mode, 1, 2 * rows * LANES), 'mode', split...  5.94 us
    ppermute x3, starting transfers between devices, shards(): lax.ppermute(table, 'dom', [(d, d // side * side + (d + i) % side) for d...  5.51 us
    ppermute x3, starting transfers between devices, shards(): lax.ppermute(table, 'dom', [(d, (d + i * side) % parts) for d in range(pa...  3.78 us
    ppermute x3, waiting for transfers between devices, shards(): lax.ppermute(table, 'dom', [(d, (d + i * side) % parts) for d in range(pa...  3.47 us
  transfers between devices with their start and end apart: 7, of which 4 were waited for; matrix products, arithmetic and copies ran while one was open for 1% of the time, Pallas kernels for 3%

profile of v8, /device:TPU:1, one launch (start us, length us, event | category | flops | bytes accessed | tf_op | source)
XLA Modules:
  0.0 84.7 jit_solution(11804325197617114289)
XLA Ops:
  0.0 2.2 %pack.1 = f32[16,96,128]{2,1,0:T(8,128)} custom-call(f32[24,2,2048]{2,1,0:T(2,128)} %bitcast.27, f32[24,2,2048]{2,1,0:T(2,128)} %bitcast.28), custom_call_target="tpu_custom_call" | custom-call | tf_op jit(solution)/shard_map/pack/pallas_call | solution.py:224
  2.2 0.0 copy-start.3
  2.2 0.0 copy-start.2
  2.2 0.0 copy-start.4
  2.2 0.0 copy-start.1
  2.2 10.1 %all-to-all-start = ((f32[16,1,12288]{2,1,0:T(1,128)}), f32[16,1,12288]{2,1,0:T(1,128)S(1)}, u32[]{:S(2)}, u32[]{:S(2)}) async-start(f32[16,1,12288]{2,1,0:T(1,128)} %bitcast.25), calls=%async_computation | async-start | bytes 1572864 | tf_op jit(solution)/shard_map/all_to_all | solution.py:230
  12.4 0.0 copy-done.3
  12.4 0.1 reshape.46
  12.4 0.1 pad.11.clone
  12.5 0.1 pad.10.clone
  12.6 0.0 copy-done.2
  12.6 0.1 copy.15
  12.7 0.1 reshape.41
  12.8 0.0 copy-start
  12.8 2.8 %collective-permute-start.1 = (f32[16,128]{1,0:T(8,128)S(1)}, f32[16,128]{1,0:T(8,128)S(1)}, u32[]{:S(2)}, u32[]{:S(2)}) collective-permute-start(f32[16,128]{1,0:T(8,128)S(1)} %get-tuple-element.14), channel_id=1, source_target_pairs={{0,2},{1,3},{2,0},{3,1},{4,6},{5,7},{6,4},{7,5},{8,10},{9,11},{10,... | collective-permute-start | bytes 24584 | tf_op jit(solution)/shard_map/ppermute | solution.py:241
  15.6 0.3 collective-permute-start
  15.9 2.4 %collective-permute-start.2 = (f32[16,128]{1,0:T(8,128)S(1)}, f32[16,128]{1,0:T(8,128)S(1)}, u32[]{:S(2)}, u32[]{:S(2)}) collective-permute-start(f32[16,128]{1,0:T(8,128)S(1)} %get-tuple-element.14), channel_id=1, source_target_pairs={{0,3},{1,0},{2,1},{3,2},{4,7},{5,4},{6,5},{7,6},{8,11},{9,8},{10,9... | collective-permute-start | bytes 24584 | tf_op jit(solution)/shard_map/ppermute | solution.py:241
  18.4 0.0 collective-permute-done.1
  18.4 1.2 %collective-permute-done = f32[16,128]{1,0:T(8,128)S(1)} collective-permute-done((f32[16,128]{1,0:T(8,128)S(1)}, f32[16,128]{1,0:T(8,128)S(1)}, u32[]{:S(2)}, u32[]{:S(2)}) %collective-permute-start) | collective-permute-done | bytes 8224 | tf_op jit(solution)/shard_map/ppermute | solution.py:241
  19.6 0.0 collective-permute-done.2
  19.6 2.7 %collective-permute-start.5 = (f32[4,16,128]{2,1,0:T(8,128)S(1)}, f32[4,16,128]{2,1,0:T(8,128)S(1)}, u32[]{:S(2)}, u32[]{:S(2)}) collective-permute-start(f32[4,16,128]{2,1,0:T(8,128)S(1)} %pad_maximum_fusion.refs_0_), channel_id=1, source_target_pairs={{0,12},{1,13},{2,14},{3,15},{4,0},{5,1},{6,2},{7,3},{8,4},{9,5},{1... | collective-permute-start | bytes 98312 | tf_op jit(solution)/shard_map/ppermute | solution.py:244
  22.4 0.3 collective-permute-start.4
  22.7 0.7 collective-permute-start.3
  23.4 0.0 copy-done.4
  23.4 0.1 pad_maximum_fusion.1.scal
  23.5 0.0 copy-done.1
  23.5 0.3 weights.1
  23.8 0.0 collective-permute-done.5.refs_3_
  23.8 3.1 %collective-permute-done.4.refs_2_ = f32[4,16,128]{2,1,0:T(8,128)S(1)} collective-permute-done((f32[4,16,128]{2,1,0:T(8,128)S(1)}, f32[4,16,128]{2,1,0:T(8,128)S(1)}, u32[]{:S(2)}, u32[]{:S(2)}) %collective-permute-start.4) | collective-permute-done | bytes 32800 | tf_op jit(solution)/shard_map/ppermute | solution.py:244
  26.9 0.4 collective-permute-done.3.refs_1_
  27.3 1.8 %prep.1.onehot = bf16[8,576,128]{2,1,0:T(8,128)(2,1)S(1)} custom-call(s32[16]{0:T(128)S(1)} %fusion.1.order, f32[4,16,128]{2,1,0:T(8,128)S(1)} %pad_maximum_fusion.refs_0_, f32[4,16,128]{2,1,0:T(8,128)S(1)} %collective-permute-done.3.refs_1_, f32[4,16,128]{2,1,0:T(8,128)S(1)} %collective-permute-done.4.refs_2_, f32[4,16,128]{2,1,0:T(8,128)S(1)} %collective-permute-done.5.refs_3_), custom_call_target="tpu_custom_call" | custom-call | bytes 8388608 | tf_op jit(solution)/shard_map/prep/pallas_call | solution.py:249
  29.1 5.9 %all-to-all-done = f32[16,1,12288]{2,1,0:T(1,128)S(1)} async-done(((f32[16,1,12288]{2,1,0:T(1,128)}), f32[16,1,12288]{2,1,0:T(1,128)S(1)}, u32[]{:S(2)}, u32[]{:S(2)}) %all-to-all-start) | async-done | bytes 786464 | tf_op jit(solution)/shard_map/all_to_all | solution.py:230
  35.1 0.0 copy-done
  35.1 1.2 %lines.1 = f32[256,1,384]{2,1,0:T(1,128)S(1)} custom-call(f32[16,96,128]{2,1,0:T(8,128)S(1)} %bitcast.22, bf16[4,256,256]{2,1,0:T(8,128)(2,1)S(1)} %copy-done), custom_call_target="tpu_custom_call" | custom-call | tf_op jit(solution)/shard_map/lines/pallas_call | solution.py:269
  36.2 27.3 %all_to_all.15 = f32[256,1,384]{2,1,0:T(1,128)S(1)} all-to-all(f32[256,1,384]{2,1,0:T(1,128)S(1)} %lines.1), channel_id=1, replica_groups=mesh['mode'=16,'dom'=16] {'dom','mode'}, dimensions={0} | all-to-all | bytes 786432 | tf_op jit(solution)/shard_map/all_to_all | solution.py:285
  63.5 8.3 %solve.1 = f32[16,3,16,128]{3,2,1,0:T(8,128)S(1)} custom-call(f32[9]{0:T(128)S(1)} %pad_maximum_fusion.1.scal, f32[256,384]{1,0:T(8,128)S(1)} %bitcast.23, bf16[8,576,128]{2,1,0:T(8,128)(2,1)S(1)} %prep.1.onehot, bf16[1152,256]{1,0:T(8,128)(2,1)S(1)} %weights.1), custom_call_target="tpu_custom_call" | custom-call | tf_op jit(solution)/shard_map/solve/pallas_call | solution.py:292
  71.8 11.9 %all_to_all.16 = f32[16,1,6144]{2,1,0:T(1,128)S(1)} all-to-all(f32[16,1,6144]{2,1,0:T(1,128)S(1)} %bitcast.24), channel_id=1, replica_groups=mesh['mode'=16,'dom'=16] {'dom'}, dimensions={0} | all-to-all | bytes 786432 | tf_op jit(solution)/shard_map/all_to_all | solution.py:301
  83.7 1.0 %reshape.45 = f32[3,8,2,2048]{3,2,1,0:T(2,128)} reshape(f32[3,8,2,16,128]{4,3,2,1,0:T(8,128)S(1)} %copy.17) | data formatting | bytes 786432 | tf_op jit(solution)/shard_map/reshape | solution.py:303
  (7 shorter events, 0.1 us)
Async XLA Ops:
  2.2 10.2 %copy-start.3 = (s32[2,8]{1,0:T(2,128)S(1)}, s32[2,8]{1,0:T(2,128)}, u32[]{:S(2)}) copy-start(s32[2,8]{1,0:T(2,128)} %param.11) | copy-start | bytes 196
  2.2 10.4 %copy-start.2 = (s32[9,32]{1,0:T(8,128)S(1)}, s32[9,32]{1,0:T(8,128)}, u32[]{:S(2)}) copy-start(s32[9,32]{1,0:T(8,128)} %param.10) | copy-start | bytes 3460
  2.2 21.2 %copy-start.4 = (f32[8]{0:T(128)S(1)}, f32[8]{0:T(128)}, u32[]{:S(2)}) copy-start(f32[8]{0:T(128)} %constant.92.clone) | copy-start | bytes 100
  2.2 21.3 %copy-start.1 = (f32[9,64,64]{2,1,0:T(8,128)S(1)}, f32[9,64,64]{2,1,0:T(8,128)}, u32[]{:S(2)}) copy-start(f32[9,64,64]{2,1,0:T(8,128)} %blocks.1) | copy-start | bytes 442372
  2.2 32.8 %all-to-all-start = ((f32[16,1,12288]{2,1,0:T(1,128)}), f32[16,1,12288]{2,1,0:T(1,128)S(1)}, u32[]{:S(2)}, u32[]{:S(2)}) async-start(f32[16,1,12288]{2,1,0:T(1,128)} %bitcast.25), calls=%async_computation | async-start | bytes 1572864 | tf_op jit(solution)/shard_map/all_to_all | solution.py:230
  12.8 22.3 %copy-start = (bf16[4,256,256]{2,1,0:T(8,128)(2,1)S(1)}, bf16[4,256,256]{2,1,0:T(8,128)(2,1)}, u32[]{:S(2)}) copy-start(bf16[4,256,256]{2,1,0:T(8,128)(2,1)} %constant.91.clone.tables) | copy-start | bytes 1572868
  12.8 5.6 %collective-permute-start.1 = (f32[16,128]{1,0:T(8,128)S(1)}, f32[16,128]{1,0:T(8,128)S(1)}, u32[]{:S(2)}, u32[]{:S(2)}) collective-permute-start(f32[16,128]{1,0:T(8,128)S(1)} %get-tuple-element.14), channel_id=1, source_target_pairs={{0,2},{1,3},{2,0},{3,1},{4,6},{5,7},{6,4},{7,5},{8,10},{9,11},{10,... | collective-permute-start | bytes 24584 | tf_op jit(solution)/shard_map/ppermute | solution.py:241
  15.6 4.0 %collective-permute-start = (f32[16,128]{1,0:T(8,128)S(1)}, f32[16,128]{1,0:T(8,128)S(1)}, u32[]{:S(2)}, u32[]{:S(2)}) collective-permute-start(f32[16,128]{1,0:T(8,128)S(1)} %get-tuple-element.14), channel_id=1, source_target_pairs={{0,1},{1,2},{2,3},{3,0},{4,5},{5,6},{6,7},{7,4},{8,9},{9,10},{10,1... | collective-permute-start | bytes 24584 | tf_op jit(solution)/shard_map/ppermute | solution.py:241
  15.9 3.7 %collective-permute-start.2 = (f32[16,128]{1,0:T(8,128)S(1)}, f32[16,128]{1,0:T(8,128)S(1)}, u32[]{:S(2)}, u32[]{:S(2)}) collective-permute-start(f32[16,128]{1,0:T(8,128)S(1)} %get-tuple-element.14), channel_id=1, source_target_pairs={{0,3},{1,0},{2,1},{3,2},{4,7},{5,4},{6,5},{7,6},{8,11},{9,8},{10,9... | collective-permute-start | bytes 24584 | tf_op jit(solution)/shard_map/ppermute | solution.py:241
  19.6 4.2 %collective-permute-start.5 = (f32[4,16,128]{2,1,0:T(8,128)S(1)}, f32[4,16,128]{2,1,0:T(8,128)S(1)}, u32[]{:S(2)}, u32[]{:S(2)}) collective-permute-start(f32[4,16,128]{2,1,0:T(8,128)S(1)} %pad_maximum_fusion.refs_0_), channel_id=1, source_target_pairs={{0,12},{1,13},{2,14},{3,15},{4,0},{5,1},{6,2},{7,3},{8,4},{9,5},{1... | collective-permute-start | bytes 98312 | tf_op jit(solution)/shard_map/ppermute | solution.py:244
  22.4 4.5 %collective-permute-start.4 = (f32[4,16,128]{2,1,0:T(8,128)S(1)}, f32[4,16,128]{2,1,0:T(8,128)S(1)}, u32[]{:S(2)}, u32[]{:S(2)}) collective-permute-start(f32[4,16,128]{2,1,0:T(8,128)S(1)} %pad_maximum_fusion.refs_0_), channel_id=1, source_target_pairs={{0,8},{1,9},{2,10},{3,11},{4,12},{5,13},{6,14},{7,15},{8,0},{9,1},... | collective-permute-start | bytes 98312 | tf_op jit(solution)/shard_map/ppermute | solution.py:244
  22.7 4.6 %collective-permute-start.3 = (f32[4,16,128]{2,1,0:T(8,128)S(1)}, f32[4,16,128]{2,1,0:T(8,128)S(1)}, u32[]{:S(2)}, u32[]{:S(2)}) collective-permute-start(f32[4,16,128]{2,1,0:T(8,128)S(1)} %pad_maximum_fusion.refs_0_), channel_id=1, source_target_pairs={{0,4},{1,5},{2,6},{3,7},{4,8},{5,9},{6,10},{7,11},{8,12},{9,13},{1... | collective-permute-start | bytes 98312 | tf_op jit(solution)/shard_map/ppermute | solution.py:244
